TPU v7x, 32 devices: a whole 2x2x4 slice. The times are simulated.
32 devices in a mesh: group: 2 (over x), wide: 16 (over z, y, core).
Axes of the slice: x: 2, y: 2, z: 4, core: 2. Of those that a mesh axis runs over, the one named last changes fastest.
Arguments:
- tokens: bfloat16 [192, 2688], P('group', 'wide'), parts along dimension 0, may hold values from -6 to 6
- mix_gain: bfloat16 [2688], replicated, may hold values from 0.099609375 to 1.8984375
- proj_inner: bfloat16 [2688, 2, 4096], P(None, None, 'wide'), may hold values from -0.125 to 0.125
- proj_maps: bfloat16 [2688, 2048], P(None, 'wide'), may hold values from -0.125 to 0.125
- proj_step: bfloat16 [2688, 64], P(None, 'wide'), may hold values from -0.125 to 0.125
- window_inner: bfloat16 [192, 3, 4096], P('group', None, 'wide'), parts along dimension 0, may hold values from -6 to 6
- window_maps: bfloat16 [192, 3, 2048], P('group', None, 'wide'), parts along dimension 0, may hold values from -6 to 6
- kernel_inner: bfloat16 [4, 4096], P(None, 'wide'), may hold values from -3 to 3
- kernel_maps: bfloat16 [4, 2048], P(None, 'wide'), may hold values from -3 to 3
- step_bias: float32 [64], P('wide'), may hold values from -4 to -1
- decay_log: float32 [64], P('wide'), may hold values from -1 to 2.5
- skip_gain: float32 [64], P('wide'), may hold values from 0.5 to 2
- gated_gain: bfloat16 [4096], P('wide'), may hold values from 0.099609375 to 1.8984375
- proj_out: bfloat16 [4096, 2688], P('wide'), may hold values from -0.125 to 0.125
- ssm_state: float32 [192, 64, 64, 128], P('group', 'wide'), parts along dimension 0, may hold values from -0.6 to 0.6
- moe_gain: bfloat16 [2688], replicated, may hold values from 0.099609375 to 1.8984375
- router_weight: bfloat16 [2688, 16], replicated, may hold values from -0.125 to 0.125
- expert_ids: int32 [192, 6], P('group'), parts along dimension 0, may hold values from 0 to 15, all different within a row; in each aligned block of 96 rows (0 to 95, 96 to 191, ...) at most 96 rows name the same one
- expert_up: bfloat16 [16, 2688, 928], P('wide'), may hold values from -0.125 to 0.125
- expert_down: bfloat16 [16, 928, 2688], P('wide'), may hold values from -0.1875 to 0.1875
Outputs:
- next_hidden: bfloat16 [192, 2688], P('group', 'wide'), parts along dimension 0
- new_state: float32 [192, 64, 64, 128], P('group', 'wide'), parts along dimension 0
There are 2 independent parts, one for each index of `group`. A program takes and returns all parts, laid end to end along the dimension named above; an argument that names none is the same for every part. Nothing has to cross between parts.
Inputs may be any that keep to these rules, and one draw needn't show every extreme that they name: `expert_ids`: each token names 6 different experts; no expert is named by more than 96 tokens of a part, a bound that some block reaches.
All inputs are finite; a program needn't handle non-finite values.
Results may differ from a plain program's by a relative error of at most 0.013.
Values may be sent and summed in bfloat16 or wider, within the bound.
A program may use at most 128 MiB of HBM per device.

v0:
```python
import functools

import jax
import jax.numpy as jnp
from jax import lax
from jax.experimental import pallas as pl
from jax.experimental.pallas import tpu as pltpu
from jax.sharding import PartitionSpec as P

HEADS = 64
HEAD_DIM = 64
STATE = 128
GROUPS = 8
EPSILON = 1e-05
MESH = pl.DeviceIdType.MESH
F32 = jnp.float32
BF16 = jnp.bfloat16


def greet_all(n, me):
    barrier = pltpu.get_barrier_semaphore()

    def greet(k, carry):
        pl.semaphore_signal(
            barrier, inc=1, device_id={"wide": lax.rem(me + k, n)}, device_id_type=MESH
        )
        return carry

    lax.fori_loop(1, n, greet, 0)


def await_all(n):
    pl.semaphore_wait(pltpu.get_barrier_semaphore(), n - 1)


def place_of(n, me):
    lines = n // 4
    return lines, me // 4, lax.rem(me // 2, 2), lax.rem(me, 2)


def index_of(line, side, core):
    return line * 4 + side * 2 + core


def gather_all(n, me, own, landing, send_sems, recv_sems, meanwhile=None):
    lines, line, side, core = place_of(n, me)
    across = index_of(line, 1 - side, core)
    partner = index_of(line, side, 1 - core)
    sent = []

    def send(src, origin, peer):
        copy = pltpu.make_async_remote_copy(
            src_ref=src,
            dst_ref=landing.at[origin],
            send_sem=send_sems.at[len(sent)],
            recv_sem=recv_sems.at[origin],
            device_id={"wide": peer},
            device_id_type=MESH,
        )
        copy.start()
        sent.append(copy)

    def arrive(origin):
        pltpu.make_async_remote_copy(
            src_ref=own,
            dst_ref=landing.at[origin],
            send_sem=send_sems.at[0],
            recv_sem=recv_sems.at[origin],
            device_id={"wide": partner},
            device_id_type=MESH,
        ).wait_recv()

    for k in range(1, lines):
        send(own, me, index_of(lax.rem(line + k, lines), side, core))
    send(own, me, across)
    send(own, me, partner)
    landing[me] = own[...]
    if meanwhile is not None:
        meanwhile()
    for k in range(1, lines):
        origin = index_of(lax.rem(line + lines - k, lines), side, core)
        arrive(origin)
        send(landing.at[origin], origin, across)
        send(landing.at[origin], origin, partner)
    for k in range(lines):
        origin = index_of(lax.rem(line + lines - k, lines), 1 - side, core)
        arrive(origin)
        send(landing.at[origin], origin, partner)
    for k in range(lines):
        for other in range(2):
            arrive(index_of(lax.rem(line + lines - k, lines), other, 1 - core))
    for copy in sent:
        copy.wait_send()


def reduce_all(n, me, blocks, bufs, meanwhile=None):
    core_in, side_out, side_in, line_out, line_in, sends, core_sem, side_sem, line_sem = bufs
    lines, line, side, core = place_of(n, me)
    across = index_of(line, 1 - side, core)
    partner = index_of(line, side, 1 - core)
    sent = []

    def copy_of(src, dst, sem, peer, number):
        return pltpu.make_async_remote_copy(
            src_ref=src,
            dst_ref=dst,
            send_sem=sends.at[number],
            recv_sem=sem,
            device_id={"wide": peer},
            device_id_type=MESH,
        )

    def send(src, dst, sem, peer):
        copy = copy_of(src, dst, sem, peer, len(sent))
        copy.start()
        sent.append(copy)

    def arrive(dst, sem):
        copy_of(dst, dst, sem, partner, 0).wait_recv()

    def ahead(k):
        return lax.rem(line + k, lines)

    for k in range(1, lines + 1):
        for turn in range(2):
            other = 1 - side if turn == 0 else side
            slot = ahead(k) * 2 + other
            send(
                blocks.at[index_of(ahead(k), other, 1 - core)],
                core_in.at[slot],
                core_sem.at[slot],
                partner,
            )

    def pair_sum(k, other):
        slot = ahead(k) * 2 + other
        arrive(core_in.at[slot], core_sem.at[slot])
        return blocks[index_of(ahead(k), other, core)].astype(F32) + core_in[slot].astype(F32)

    def second(k):
        slot = ahead(k)
        side_out[slot] = pair_sum(k, 1 - side).astype(BF16)
        send(side_out.at[slot], side_in.at[slot], side_sem.at[slot], across)

    def third(k):
        slot = ahead(k)
        value = pair_sum(k, side)
        arrive(side_in.at[slot], side_sem.at[slot])
        value = value + side_in[slot].astype(F32)
        if k == lines:
            return value
        line_out[slot] = value.astype(BF16)
        send(
            line_out.at[slot],
            line_in.at[line],
            line_sem.at[line],
            index_of(slot, side, core),
        )

    second(1)
    for k in range(1, lines):
        second(k + 1)
        third(k)
    if meanwhile is not None:
        meanwhile()
    total = third(lines)
    for k in range(1, lines):
        slot = lax.rem(line + lines - k, lines)
        arrive(line_in.at[slot], line_sem.at[slot])
        total = total + line_in[slot].astype(F32)
    for copy in sent:
        copy.wait_send()
    return total


LANES = 128


def packed_shape(width, seqs):
    gap = LANES - seqs
    if gap <= 0 or seqs % gap:
        return width, 0, 0
    chunks = seqs // gap
    rest = width // (chunks + 1) // 8 * 8
    return width - rest, rest, gap


def pack_into(target, source):
    width, seqs = source.shape
    kept, rest, gap = packed_shape(width, seqs)
    target[:, :seqs] = source[:kept, :]
    if rest:
        for c in range(seqs // gap):
            target[c * rest : (c + 1) * rest, seqs:] = source[kept:, c * gap : (c + 1) * gap]


def unpack_into(target, value):
    width, seqs = target.shape
    kept, rest, gap = packed_shape(width, seqs)
    target[:kept, :] = value[:, :seqs]
    if rest:
        for c in range(seqs // gap):
            target[kept:, c * gap : (c + 1) * gap] = value[c * rest : (c + 1) * rest, seqs:]


def gather_kernel(
    n,
    local_heads,
    tokens,
    gain,
    weights_hbm,
    window,
    taps,
    step_weights,
    normed_out,
    in_out,
    out_out,
    step_out,
    landing,
    full,
    packing,
    own,
    weights,
    mapped,
    arrived,
    weight_sem,
    send_sems,
    recv_sems,
    map_send,
    map_recv,
):
    me = lax.axis_index("wide")
    width = tokens.shape[0]
    cols = window.shape[2]
    load = pltpu.make_async_copy(weights_hbm, weights, weight_sem)
    load.start()
    greet_all(n, me)
    full[:width, :] = tokens[...].astype(F32)
    packing[...] = jnp.zeros_like(packing)
    pack_into(packing, full.at[:width, :])
    own[...] = packing[...].astype(BF16)
    await_all(n)
    gather_all(n, me, own, landing, send_sems, recv_sems)
    for i in range(n):
        unpack_into(full.at[i * width : (i + 1) * width, :], landing[i].astype(F32))
    values = full[...]
    mean = jnp.mean(values * values, axis=0, keepdims=True)
    scaled = (values * lax.rsqrt(mean + EPSILON)).T
    normed = (scaled * gain[...].astype(F32)[None]).astype(BF16)
    normed_out[...] = normed
    load.wait()
    raw = jnp.dot(normed, weights[...], preferred_element_type=F32).astype(BF16).astype(F32)
    kernel = taps[...].astype(F32)
    mixed = raw * kernel[3:4]
    for k in range(3):
        mixed = mixed + window[k].astype(F32) * kernel[k : k + 1]
    mapped[...] = (mixed * jax.nn.sigmoid(mixed)).astype(BF16)
    half = n // 2
    per_group = half // GROUPS
    readers = HEADS // GROUPS // local_heads
    kind = me // half
    own_group = lax.rem(me, half) // per_group
    own_slot = kind * per_group + lax.rem(me, per_group)

    def send(r):
        peer = own_group * readers + r
        return peer, pltpu.make_async_remote_copy(
            src_ref=mapped,
            dst_ref=arrived.at[own_slot],
            send_sem=map_send.at[r],
            recv_sem=map_recv.at[own_slot],
            device_id={"wide": peer},
            device_id_type=MESH,
        )

    for r in range(readers):
        peer, copy = send(r)

        @pl.when(peer != me)
        def _():
            copy.start()

        @pl.when(peer == me)
        def _():
            arrived[own_slot] = mapped[...]

    step_out[...] = lax.dot_general(
        normed, step_weights[...], (((1,), (1,)), ((), ())), preferred_element_type=F32
    ).astype(BF16)
    group = me // readers
    for slot in range(2 * per_group):
        origin = (slot // per_group) * half + group * per_group + slot % per_group

        @pl.when(origin != me)
        def _():
            pltpu.make_async_remote_copy(
                src_ref=mapped,
                dst_ref=arrived.at[slot],
                send_sem=map_send.at[0],
                recv_sem=map_recv.at[slot],
                device_id={"wide": me},
                device_id_type=MESH,
            ).wait_recv()

    for slot in range(per_group):
        in_out[:, slot * cols : (slot + 1) * cols] = arrived[slot].astype(F32)
        out_out[:, slot * cols : (slot + 1) * cols] = arrived[per_group + slot].astype(F32)
    for r in range(readers):
        peer, copy = send(r)

        @pl.when(peer != me)
        def _():
            copy.wait_send()


def state_kernel(
    rows,
    heads,
    both,
    window,
    taps,
    step_raw,
    step_bias,
    decay_log,
    skip_gain,
    state,
    in_maps,
    out_maps,
    new_state,
    gated,
):
    inner = heads * HEAD_DIM
    head_ids = lax.broadcasted_iota(jnp.int32, (1, inner), 1) // HEAD_DIM

    def spread(ref):
        wide = jnp.zeros((1, inner), F32)
        for h in range(heads):
            wide = jnp.where(head_ids == h, ref[h], wide)
        return wide

    kernel = taps[...].astype(F32)
    mixed = both[:, inner:].astype(F32) * kernel[3:4]
    for k in range(3):
        mixed = mixed + window[k].astype(F32) * kernel[k : k + 1]
    inputs = (mixed * jax.nn.sigmoid(mixed)).astype(BF16).astype(F32)
    raw = step_raw[...].astype(F32)
    steps = jnp.zeros((rows, inner), F32)
    for h in range(heads):
        steps = jnp.where(head_ids == h, raw[:, h : h + 1], steps)
    steps = jax.nn.softplus(steps + spread(step_bias))
    decays = jnp.exp(-jnp.exp(spread(decay_log)) * steps).T
    columns = (steps * inputs).T
    readers = out_maps[...].astype(BF16)
    row_ids = lax.broadcasted_iota(jnp.int32, (rows, inner), 0)
    total = jnp.zeros((rows, inner), F32)
    for j in range(rows):
        maps = in_maps[j : j + 1, :]
        parts = []
        for h in range(heads):
            part = slice(h * HEAD_DIM, (h + 1) * HEAD_DIM)
            fresh = decays[part, j : j + 1] * state[j, h] + columns[part, j : j + 1] * maps
            new_state[j, h] = fresh
            parts.append(fresh.astype(BF16))
        block = jnp.concatenate(parts, axis=0)
        found = lax.dot_general(
            readers, block, (((1,), (1,)), ((), ())), preferred_element_type=F32
        )
        total = jnp.where(row_ids == j, found, total)
    readout = total + spread(skip_gain) * inputs
    gate = both[:, :inner].astype(F32)
    gated[...] = readout * (gate * jax.nn.sigmoid(gate))


def expert_kernel(
    n,
    partners,
    gated,
    gated_gain,
    proj_out,
    tokens,
    moe_gain,
    router,
    expert_ids,
    up_hbm,
    down_hbm,
    result,
    up,
    down,
    terms,
    gains,
    router_hi,
    router_lo,
    packing,
    own,
    outgoing,
    hidden_own,
    hidden_all,
    squares,
    squares_in,
    load_sems,
    square_send,
    square_recv,
    hid_send,
    hid_recv,
    *bufs,
):
    me = lax.axis_index("wide")
    width, seqs = tokens.shape
    load_up = pltpu.make_async_copy(up_hbm, up, load_sems.at[0])
    load_down = pltpu.make_async_copy(down_hbm, down, load_sems.at[1])
    load_up.start()
    load_down.start()
    greet_all(n, me)
    values = gated[...]
    own_squares = jnp.sum(values * values, axis=1, keepdims=True)
    squares[...] = jnp.broadcast_to(own_squares, squares.shape)
    packing[...] = jnp.zeros_like(packing)
    own[...] = jnp.zeros_like(own)
    terms[:width, :] = tokens[...].astype(F32)
    pack_into(own, terms.at[:width, :])
    await_all(n)
    first = (me // partners) * partners
    place = lax.rem(me, partners)

    def partner_copy(k):
        other = lax.rem(place + k, partners)
        return pltpu.make_async_remote_copy(
            src_ref=squares,
            dst_ref=squares_in.at[k - 1],
            send_sem=square_send.at[k - 1],
            recv_sem=square_recv.at[k - 1],
            device_id={"wide": first + other},
            device_id_type=MESH,
        )

    for k in range(1, partners):
        partner_copy(k).start()
    weighted = (values * gated_gain[...].astype(F32)[None]).astype(BF16)
    mixed = jnp.dot(weighted, proj_out[...], preferred_element_type=F32)
    total = own_squares
    for k in range(1, partners):
        partner_copy(k).wait()
        total = total + squares_in[k - 1][:, :1]
    channels = values.shape[1] * partners
    terms[...] = (mixed * lax.rsqrt(total / channels + EPSILON)).T
    for i in range(n):
        pack_into(packing.at[i], terms.at[i * width : (i + 1) * width, :])
        outgoing[i] = packing[i].astype(BF16)

    def prepare():
        gain = moe_gain[...].astype(F32)[None]
        gains[...] = jnp.broadcast_to(gain, (seqs, gain.shape[1])).T
        folded = router[...].astype(F32) * gain
        high = folded.astype(BF16)
        router_hi[...] = high
        router_lo[...] = (folded - high.astype(F32)).astype(BF16)

    half = len(bufs) // 2
    reduced = reduce_all(n, me, outgoing, bufs[:half], prepare)
    hidden_own[...] = (own[...] + reduced).astype(BF16)
    gather_all(n, me, hidden_own, hidden_all, hid_send, hid_recv)
    for i in range(n):
        unpack_into(terms.at[i * width : (i + 1) * width, :], hidden_all[i].astype(F32))
    values = terms[...]
    mean = jnp.mean(values * values, axis=0, keepdims=True)
    moe_scale = lax.rsqrt(mean + EPSILON)
    rounded = values.astype(BF16)
    moe_input = (values * moe_scale * gains[...]).astype(BF16)
    load_up.wait()
    units = jnp.dot(up[0], moe_input, preferred_element_type=F32)
    logits = moe_scale * (
        jnp.dot(router_hi[...], rounded, preferred_element_type=F32)
        + jnp.dot(router_lo[...], rounded, preferred_element_type=F32)
    )
    expert = lax.broadcasted_iota(jnp.int32, logits.shape, 0)
    named = jnp.zeros(logits.shape, F32)
    for k in range(expert_ids.shape[0]):
        named = named + jnp.where(expert == expert_ids[k : k + 1, :], 1.0, 0.0)
    score = named * jax.nn.sigmoid(logits)
    mine = jnp.sum(jnp.where(expert == me, score, 0.0), axis=0, keepdims=True)
    weight = mine / jnp.sum(score, axis=0, keepdims=True)
    active = jnp.square(jnp.maximum(units, 0.0)).T.astype(BF16)
    load_down.wait()
    served = jnp.dot(active, down[0], preferred_element_type=F32)
    terms[...] = served.T.astype(BF16).astype(F32) * weight
    for i in range(n):
        pack_into(packing.at[i], terms.at[i * width : (i + 1) * width, :])
        outgoing[i] = packing[i].astype(BF16)
    reduced = reduce_all(n, me, outgoing, bufs[half:])
    unpack_into(terms.at[:width, :], hidden_own[...].astype(F32) + reduced)
    result[...] = terms[:width, :].astype(BF16)


def vmem(count):
    return [pl.BlockSpec(memory_space=pltpu.VMEM)] * count


ANY = pl.BlockSpec(memory_space=pl.ANY)
DMA = pltpu.SemaphoreType.DMA


def local(
    n,
    tokens,
    mix_gain,
    proj_inner,
    proj_maps,
    proj_step,
    window_inner,
    window_maps,
    kernel_inner,
    kernel_maps,
    step_bias,
    decay_log,
    skip_gain,
    gated_gain,
    proj_out,
    ssm_state,
    moe_gain,
    router_weight,
    expert_ids,
    expert_up,
    expert_down,
):
    seqs, width = tokens.shape
    full_width = proj_inner.shape[0]
    inner = proj_inner.shape[2]
    cols = proj_maps.shape[1]
    heads = proj_step.shape[1]
    readers = HEADS // GROUPS // heads
    slots = 2 * (STATE // cols)
    kept = packed_shape(width, seqs)[0]
    normed, in_maps, out_maps, step_raw = pl.pallas_call(
        functools.partial(gather_kernel, n, heads),
        out_shape=(
            jax.ShapeDtypeStruct((seqs, full_width), BF16),
            jax.ShapeDtypeStruct((seqs, STATE), F32),
            jax.ShapeDtypeStruct((seqs, STATE), F32),
            jax.ShapeDtypeStruct((seqs, heads), BF16),
        ),
        in_specs=vmem(2) + [ANY] + vmem(3),
        out_specs=tuple(vmem(4)),
        scratch_shapes=[
            pltpu.VMEM((n, kept, LANES), BF16),
            pltpu.VMEM((full_width, seqs), F32),
            pltpu.VMEM((kept, LANES), F32),
            pltpu.VMEM((kept, LANES), BF16),
            pltpu.VMEM((full_width, cols), BF16),
            pltpu.VMEM((seqs, cols), BF16),
            pltpu.VMEM((slots, seqs, cols), BF16),
            DMA(()),
            DMA((n,)),
            DMA((n,)),
            DMA((readers,)),
            DMA((slots,)),
        ],
        compiler_params=pltpu.CompilerParams(
            collective_id=0, has_side_effects=True, vmem_limit_bytes=54 << 20
        ),
        cost_estimate=pl.CostEstimate(
            flops=2 * seqs * full_width * cols, bytes_accessed=40 << 20, transcendentals=0
        ),
        name="gather_tokens",
    )(tokens.T, mix_gain, proj_maps, window_maps.transpose(1, 0, 2), kernel_maps, proj_step.T)
    both = jnp.dot(
        normed, proj_inner.reshape(full_width, 2 * inner), preferred_element_type=F32
    ).astype(BF16)
    rows = 16
    by_row = lambda i: (i, 0)
    by_state = lambda i: (i, 0, 0, 0)
    scalars = pl.BlockSpec(memory_space=pltpu.SMEM)
    new_state, gated = pl.pallas_call(
        functools.partial(state_kernel, rows, heads),
        grid=(seqs // rows,),
        out_shape=(
            jax.ShapeDtypeStruct(ssm_state.shape, F32),
            jax.ShapeDtypeStruct((seqs, inner), F32),
        ),
        in_specs=[
            pl.BlockSpec((rows, 2 * inner), by_row),
            pl.BlockSpec((3, rows, inner), lambda i: (0, i, 0)),
            pl.BlockSpec(kernel_inner.shape, lambda i: (0, 0)),
            pl.BlockSpec((rows, heads), by_row),
            scalars,
            scalars,
            scalars,
            pl.BlockSpec((rows, heads, HEAD_DIM, STATE), by_state),
            pl.BlockSpec((rows, STATE), by_row),
            pl.BlockSpec((rows, STATE), by_row),
        ],
        out_specs=(
            pl.BlockSpec((rows, heads, HEAD_DIM, STATE), by_state),
            pl.BlockSpec((rows, inner), by_row),
        ),
        compiler_params=pltpu.CompilerParams(vmem_limit_bytes=54 << 20),
        name="update_state",
    )(
        both,
        window_inner.transpose(1, 0, 2),
        kernel_inner,
        step_raw,
        step_bias,
        decay_log,
        skip_gain,
        ssm_state,
        in_maps,
        out_maps,
    )
    lines = n // 4

    def piece(count):
        return pltpu.VMEM((count, kept, LANES), BF16)

    reduce_bufs = [
        piece(2 * lines),
        piece(lines),
        piece(lines),
        piece(lines),
        piece(lines),
        DMA((4 * lines - 1,)),
        DMA((2 * lines,)),
        DMA((lines,)),
        DMA((lines,)),
    ]
    up_shape = (1, expert_up.shape[2], full_width)
    next_hidden = pl.pallas_call(
        functools.partial(expert_kernel, n, readers),
        out_shape=jax.ShapeDtypeStruct((width, seqs), BF16),
        in_specs=vmem(7) + [ANY, ANY],
        out_specs=vmem(1)[0],
        scratch_shapes=[
            pltpu.VMEM(up_shape, BF16),
            pltpu.VMEM(expert_down.shape, BF16),
            pltpu.VMEM((full_width, seqs), F32),
            pltpu.VMEM((full_width, seqs), F32),
            pltpu.VMEM((router_weight.shape[1], full_width), BF16),
            pltpu.VMEM((router_weight.shape[1], full_width), BF16),
            pltpu.VMEM((n, kept, LANES), F32),
            pltpu.VMEM((kept, LANES), F32),
            piece(n),
            pltpu.VMEM((kept, LANES), BF16),
            piece(n),
            pltpu.VMEM((seqs, 128), F32),
            pltpu.VMEM((readers - 1, seqs, 128), F32),
            DMA((2,)),
            DMA((readers - 1,)),
            DMA((readers - 1,)),
            DMA((n,)),
            DMA((n,)),
        ]
        + reduce_bufs * 2,
        compiler_params=pltpu.CompilerParams(
            collective_id=1, has_side_effects=True, vmem_limit_bytes=60 << 20
        ),
        name="mix_and_serve",
    )(
        gated,
        gated_gain,
        proj_out,
        tokens.T,
        moe_gain,
        router_weight.T,
        expert_ids.T,
        expert_up.swapaxes(1, 2),
        expert_down,
    )
    return (next_hidden.T, new_state)


def solution(mesh):
    in_specs = (
        P("group", "wide"),
        P(),
        P(None, None, "wide"),
        P(None, "wide"),
        P(None, "wide"),
        P("group", None, "wide"),
        P("group", None, "wide"),
        P(None, "wide"),
        P(None, "wide"),
        P("wide"),
        P("wide"),
        P("wide"),
        P("wide"),
        P("wide", None),
        P("group", "wide", None, None),
        P(),
        P(),
        P("group", None),
        P("wide", None, None),
        P("wide", None, None),
    )
    out_specs = (P("group", "wide"), P("group", "wide", None, None))
    body = functools.partial(local, mesh.shape["wide"])
    return jax.shard_map(body, mesh=mesh, in_specs=in_specs, out_specs=out_specs, check_vma=False)
```

profile of v0, /device:TPU:0, one launch (start us, length us, event | category | flops | bytes accessed | tf_op | source)
XLA Modules:
  0.0 82.6 jit_solution(5654770988122193748)
XLA Ops:
  0.6 20.8 %gather_tokens.1 = (bf16[96,2688]{1,0:T(8,128)(2,1)}, f32[96,128]{1,0:T(8,128)}, f32[96,128]{1,0:T(8,128)}, bf16[96,4]{1,0:T(8,128)(2,1)}) custom-call(bf16[168,96]{1,0:T(8,128)(2,1)} %bitcast.16, bf16[2688]{0:T(1024)(128)(2,1)} %gain.1, bf16[2688,128]{1,0:T(8,128)(2,1)} %weights_hbm.1, bf16[3,96,128]{2,1,0:T(8,128)(2,1)} %bitcast.20, bf16[4,128]{1,0:T(4,128)(2,1)} %taps.2, ...), custom_call_target="tpu_custom_call" | custom-call | flops 66060288 | bytes 41943040 | tf_op jit(solution)/shard_map/gather_tokens/pallas_call | solution.py:533
  21.4 0.0 copy-start
  21.5 2.3 %copy.22 = bf16[336,8,2,256]{3,1,2,0:T(8,128)(2,1)S(1)} copy(bf16[336,8,2,256]{3,2,1,0:T(2,128)(2,1)} %bitcast.14) | data formatting | bytes 5505024
  23.7 0.0 copy-done
  23.8 1.2 %convolution_convert_fusion.both = bf16[96,512]{1,0:T(8,128)(2,1)} fusion(bf16[96,2688]{1,0:T(8,128)(2,1)S(1)} %copy-done, bf16[2688,512]{1,0:T(8,128)(2,1)S(1)} %bitcast.12), kind=kOutput, calls=%fused_computation | convolution fusion | flops 264290304 | bytes 3366912 | tf_op jit(solution)/shard_map/dot_general | solution.py:565
  25.0 13.9 %update_state.1 = (f32[96,4,64,128]{3,2,1,0:T(8,128)}, f32[96,256]{1,0:T(8,128)}) custom-call(bf16[96,512]{1,0:T(8,128)(2,1)} %convolution_convert_fusion.both, bf16[3,96,256]{2,1,0:T(8,128)(2,1)} %bitcast.18, bf16[4,256]{1,0:T(4,128)(2,1)} %taps.3, bf16[96,4]{1,0:T(8,128)(2,1)} %get-tuple-element.9.step_raw, f32[4]{0:T(128)} %step_bias.1, f32[4]{0:T(128)} %decay_log.1, ...), custom_call_target="tpu_custom_call" | custom-call | tf_op jit(solution)/shard_map/update_state/pallas_call | solution.py:572
  38.8 42.3 %mix_and_serve.1 = bf16[168,96]{1,0:T(8,128)(2,1)} custom-call(f32[96,256]{1,0:T(8,128)} %get-tuple-element.12.gated, bf16[256]{0:T(256)(128)(2,1)} %gated_gain.1, bf16[256,2688]{1,0:T(8,128)(2,1)} %proj_out.1, bf16[168,96]{1,0:T(8,128)(2,1)} %bitcast.17, bf16[2688]{0:T(1024)(128)(2,1)} %moe_gain.1, bf16[16,2688]{1,0:T(8,128)(2,1)} %bitcast.19, ...), custom_call_target="tpu_custom_call" | custom-call | tf_op jit(solution)/shard_map/mix_and_serve/pallas_call | solution.py:626
  81.2 1.4 %copy.24 = bf16[96,168]{0,1:T(8,128)(2,1)} copy(bf16[96,168]{0,1:T(8,128)(2,1)} %bitcast.15) | data formatting | bytes 64512
Async XLA Ops:
  21.4 2.3 %copy-start = (bf16[96,2688]{1,0:T(8,128)(2,1)S(1)}, bf16[96,2688]{1,0:T(8,128)(2,1)}, u32[]{:S(2)}) copy-start(bf16[96,2688]{1,0:T(8,128)(2,1)} %get-tuple-element.8) | copy-start | bytes 1548292
where the time goes:
time: 83 us; the launch traced here: 82.6 us
  Pallas kernels  77 us (93%)
  local copies, waits for them, and re-layouts  3.7 us (4%)
  matrix products  1.21 us (1%)
    pallas_call x1, Pallas kernels, local(): pl.pallas_call(functools.partial(expert_kernel, n, readers), out_shape=ja...  42.3 us
    pallas_call x1, Pallas kernels, local(): pl.pallas_call(functools.partial(gather_kernel, n, heads), out_shape=(jax...  20.8 us
    pallas_call x1, Pallas kernels, local(): pl.pallas_call(functools.partial(state_kernel, rows, heads), grid=(seqs /...  13.9 us
    unnamed x4, local copies, waits for them, and re-layouts  3.7 us

commit v1 on v0

v1 whole, which is shorter than its diff:
```python
import functools

import jax
import jax.numpy as jnp
from jax import lax
from jax.experimental import pallas as pl
from jax.experimental.pallas import tpu as pltpu
from jax.sharding import PartitionSpec as P

HEADS = 64
HEAD_DIM = 64
STATE = 128
GROUPS = 8
EPSILON = 1e-05
MESH = pl.DeviceIdType.MESH
F32 = jnp.float32
BF16 = jnp.bfloat16


def greet_all(n, me):
    barrier = pltpu.get_barrier_semaphore()

    def greet(k, carry):
        pl.semaphore_signal(
            barrier, inc=1, device_id={"wide": lax.rem(me + k, n)}, device_id_type=MESH
        )
        return carry

    lax.fori_loop(1, n, greet, 0)


def await_all(n):
    pl.semaphore_wait(pltpu.get_barrier_semaphore(), n - 1)


def place_of(n, me):
    lines = n // 4
    return lines, me // 4, lax.rem(me // 2, 2), lax.rem(me, 2)


def index_of(line, side, core):
    return line * 4 + side * 2 + core


def gather_all(n, me, own, landing, send_sems, recv_sems, consume, meanwhile=None):
    lines, line, side, core = place_of(n, me)
    across = index_of(line, 1 - side, core)
    partner = index_of(line, side, 1 - core)
    sent = []

    def send(src, origin, peer):
        copy = pltpu.make_async_remote_copy(
            src_ref=src,
            dst_ref=landing.at[origin],
            send_sem=send_sems.at[len(sent)],
            recv_sem=recv_sems.at[origin],
            device_id={"wide": peer},
            device_id_type=MESH,
        )
        copy.start()
        sent.append(copy)

    def arrive(origin):
        pltpu.make_async_remote_copy(
            src_ref=own,
            dst_ref=landing.at[origin],
            send_sem=send_sems.at[0],
            recv_sem=recv_sems.at[origin],
            device_id={"wide": partner},
            device_id_type=MESH,
        ).wait_recv()

    for k in range(1, lines):
        send(own, me, index_of(lax.rem(line + k, lines), side, core))
    send(own, me, across)
    send(own, me, partner)
    if meanwhile is not None:
        meanwhile()
    consume(own, me)
    arrive(partner)
    consume(landing.at[partner], partner)
    for k in range(1, lines):
        origin = index_of(lax.rem(line + lines - k, lines), side, core)
        arrive(origin)
        send(landing.at[origin], origin, across)
        send(landing.at[origin], origin, partner)
        consume(landing.at[origin], origin)
    for k in range(lines):
        origin = index_of(lax.rem(line + lines - k, lines), 1 - side, core)
        arrive(origin)
        send(landing.at[origin], origin, partner)
        consume(landing.at[origin], origin)
    for other in (side, 1 - side):
        for k in range(lines):
            if k == 0 and other is side:
                continue
            origin = index_of(lax.rem(line + lines - k, lines), other, 1 - core)
            arrive(origin)
            consume(landing.at[origin], origin)
    for copy in sent:
        copy.wait_send()


def reduce_all(n, me, blocks, bufs, meanwhile=None):
    core_in, side_out, side_in, line_out, line_in, sends, core_sem, side_sem, line_sem = bufs
    lines, line, side, core = place_of(n, me)
    across = index_of(line, 1 - side, core)
    partner = index_of(line, side, 1 - core)
    sent = []

    def copy_of(src, dst, sem, peer, number):
        return pltpu.make_async_remote_copy(
            src_ref=src,
            dst_ref=dst,
            send_sem=sends.at[number],
            recv_sem=sem,
            device_id={"wide": peer},
            device_id_type=MESH,
        )

    def send(src, dst, sem, peer):
        copy = copy_of(src, dst, sem, peer, len(sent))
        copy.start()
        sent.append(copy)

    def arrive(dst, sem):
        copy_of(dst, dst, sem, partner, 0).wait_recv()

    def ahead(k):
        return lax.rem(line + k, lines)

    for k in range(1, lines + 1):
        for turn in range(2):
            other = 1 - side if turn == 0 else side
            slot = ahead(k) * 2 + other
            send(
                blocks.at[index_of(ahead(k), other, 1 - core)],
                core_in.at[slot],
                core_sem.at[slot],
                partner,
            )

    def pair_sum(k, other):
        slot = ahead(k) * 2 + other
        arrive(core_in.at[slot], core_sem.at[slot])
        return blocks[index_of(ahead(k), other, core)].astype(F32) + core_in[slot].astype(F32)

    def second(k):
        slot = ahead(k)
        side_out[slot] = pair_sum(k, 1 - side).astype(BF16)
        send(side_out.at[slot], side_in.at[slot], side_sem.at[slot], across)

    def third(k):
        slot = ahead(k)
        value = pair_sum(k, side)
        arrive(side_in.at[slot], side_sem.at[slot])
        value = value + side_in[slot].astype(F32)
        if k == lines:
            return value
        line_out[slot] = value.astype(BF16)
        send(
            line_out.at[slot],
            line_in.at[line],
            line_sem.at[line],
            index_of(slot, side, core),
        )

    second(1)
    for k in range(1, lines):
        second(k + 1)
        third(k)
    if meanwhile is not None:
        meanwhile()
    total = third(lines)
    for k in range(1, lines):
        slot = lax.rem(line + lines - k, lines)
        arrive(line_in.at[slot], line_sem.at[slot])
        total = total + line_in[slot].astype(F32)
    for copy in sent:
        copy.wait_send()
    return total


LANES = 128


def packed_shape(width, seqs):
    gap = LANES - seqs
    if gap <= 0 or seqs % gap:
        return width, 0, 0
    chunks = seqs // gap
    rest = width // (chunks + 1) // 8 * 8
    return width - rest, rest, gap


def pack_into(target, source):
    width, seqs = source.shape
    kept, rest, gap = packed_shape(width, seqs)
    target[:, :seqs] = source[:kept, :]
    if rest:
        for c in range(seqs // gap):
            target[c * rest : (c + 1) * rest, seqs:] = source[kept:, c * gap : (c + 1) * gap]


def unpack_into(target, value):
    width, seqs = target.shape
    kept, rest, gap = packed_shape(width, seqs)
    target[:kept, :] = value[:, :seqs]
    if rest:
        for c in range(seqs // gap):
            target[kept:, c * gap : (c + 1) * gap] = value[c * rest : (c + 1) * rest, seqs:]


def lane_ids(rows):
    return lax.broadcasted_iota(jnp.int32, (rows, LANES), 1)


def pack(value, seqs, extra=()):
    kept, rest, gap = packed_shape(value.shape[0], seqs)
    tail = value[kept:, :]
    pieces = [pltpu.roll(tail, seqs - c * gap, 1) for c in range(seqs // gap)]
    pieces += [pltpu.roll(row, seqs - c * gap, 1) for row in extra for c in range(seqs // gap)]
    spare = kept - sum(piece.shape[0] for piece in pieces)
    if spare:
        pieces.append(jnp.zeros((spare, LANES), F32))
    return jnp.where(lane_ids(kept) < seqs, value[:kept], jnp.concatenate(pieces, axis=0))


def unpack(value, width, seqs):
    kept, rest, gap = packed_shape(width, seqs)
    chunk = lane_ids(rest) // gap
    tail = jnp.zeros((rest, LANES), F32)
    for c in range(seqs // gap):
        piece = pltpu.roll(value[c * rest : (c + 1) * rest], LANES - seqs + c * gap, 1)
        tail = jnp.where(chunk == c, piece, tail)
    return jnp.concatenate([value[:kept], tail], axis=0)


def extra_rows(width, seqs):
    kept, rest, gap = packed_shape(width, seqs)
    first = rest * (seqs // gap)
    return first, first + 2 * (seqs // gap)


def own_columns(vector, n, me, width):
    whole = vector[...].astype(F32)[None]
    row = jnp.zeros((1, width), F32)
    for i in range(n):
        row = jnp.where(me == i, whole[:, i * width : (i + 1) * width], row)
    return jnp.broadcast_to(row, (LANES, width)).T


def padded(value):
    rows, lanes = value.shape
    return jnp.concatenate([value, jnp.zeros((rows, LANES - lanes), F32)], axis=1)


def halves(value):
    high = value.astype(BF16).astype(F32)
    return high, value - high


def convolved(fresh, window, kernel):
    mixed = fresh * kernel[3:4]
    for k in range(3):
        mixed = mixed + window[k].astype(F32) * kernel[k : k + 1]
    return (mixed * jax.nn.sigmoid(mixed)).astype(BF16).astype(F32)


def gather_kernel(
    n,
    tokens,
    gain,
    inner_hbm,
    maps_hbm,
    step_weights,
    window,
    window_maps,
    taps,
    taps_maps,
    step_bias,
    decay_log,
    skip_gain,
    state_hbm,
    state,
    columns_out,
    decays_out,
    skips_out,
    gates_out,
    in_out,
    out_out,
    landing,
    own,
    raw_inner,
    raw_maps,
    weights,
    total,
    squares,
    mapped,
    arrived,
    load_sems,
    send_sems,
    recv_sems,
    map_send,
    map_recv,
):
    me = lax.axis_index("wide")
    width, seqs = tokens.shape
    inner = window.shape[2]
    cols = window_maps.shape[2]
    heads = step_weights.shape[0]
    load_inner = pltpu.make_async_copy(inner_hbm, raw_inner, load_sems.at[0])
    load_maps = pltpu.make_async_copy(maps_hbm, raw_maps, load_sems.at[1])
    load_state = pltpu.make_async_copy(state_hbm, state, load_sems.at[2])
    load_inner.start()
    load_maps.start()
    load_state.start()
    greet_all(n, me)
    values = padded(tokens[...].astype(F32))
    sums = jnp.sum(values * values, axis=0, keepdims=True)
    scaled = values * own_columns(gain, n, me, width)
    own[...] = pack(scaled, seqs, halves(sums)).astype(BF16)
    total[...] = jnp.zeros_like(total)
    squares[...] = jnp.zeros_like(squares)
    first, last = extra_rows(width, seqs)

    def prepare():
        load_inner.wait()
        load_maps.wait()
        steps = step_weights[...].astype(F32).T.astype(BF16)
        place = lax.broadcasted_iota(jnp.int32, (2 * width, 2 * width), 0)
        wanted = jnp.where(place < width, 2 * place, 2 * (place - width) + 1)
        found = lax.broadcasted_iota(jnp.int32, (2 * width, 2 * width), 1)
        picks = jnp.where(wanted == found, 1.0, 0.0).astype(BF16)
        for i in range(n):
            rows = slice(i * width, (i + 1) * width)
            weights[i, :, :cols] = raw_maps[rows, :]
            weights[i, :, cols : cols + heads] = steps[rows, :]
            pairs = raw_inner[rows].reshape(2 * width, inner)
            split = jnp.dot(picks, pairs, preferred_element_type=F32).astype(BF16)
            for j in range(2):
                at = LANES * 2 + j * inner
                weights[i, :, at : at + inner] = split[j * width : (j + 1) * width]

    def consume(block, origin):
        value = block[...].astype(F32)
        squares[...] += value[first:last]
        fresh = unpack(value, width, seqs)[:, :seqs].astype(BF16)
        total[...] += lax.dot_general(
            fresh, weights[origin], (((0,), (0,)), ((), ())), preferred_element_type=F32
        )

    await_all(n)
    gather_all(n, me, own, landing, send_sems, recv_sems, consume, prepare)
    chunks = (last - first) // 2
    gap = seqs // chunks
    turned = jnp.concatenate([squares[...], jnp.zeros((LANES - last + first, LANES), F32)], axis=0).T
    pieces = [
        turned[seqs:, c : c + 1] + turned[seqs:, chunks + c : chunks + c + 1] for c in range(chunks)
    ]
    mean = jnp.concatenate(pieces, axis=0) / (n * width)
    scale = lax.rsqrt(mean + EPSILON)

    def projected(at, count):
        return (total[:, at : at + count] * scale).astype(BF16).astype(F32)

    mapped[...] = convolved(projected(0, cols), window_maps, taps_maps[...].astype(F32)).astype(BF16)
    half = n // 2
    per_group = half // GROUPS
    readers = HEADS // GROUPS // heads
    kind = me // half
    own_group = lax.rem(me, half) // per_group
    own_slot = kind * per_group + lax.rem(me, per_group)

    def send(r):
        peer = own_group * readers + r
        return peer, pltpu.make_async_remote_copy(
            src_ref=mapped,
            dst_ref=arrived.at[own_slot],
            send_sem=map_send.at[r],
            recv_sem=map_recv.at[own_slot],
            device_id={"wide": peer},
            device_id_type=MESH,
        )

    for r in range(readers):
        peer, copy = send(r)

        @pl.when(peer != me)
        def _():
            copy.start()

        @pl.when(peer == me)
        def _():
            arrived[own_slot] = mapped[...]

    head_ids = lax.broadcasted_iota(jnp.int32, (1, inner), 1) // HEAD_DIM

    def spread(ref):
        wide = jnp.zeros((1, inner), F32)
        for h in range(heads):
            wide = jnp.where(head_ids == h, ref[h], wide)
        return wide

    gate = projected(2 * LANES, inner)
    inputs = convolved(projected(2 * LANES + inner, inner), window, taps[...].astype(F32))
    raw = projected(cols, heads)
    steps = jnp.zeros((seqs, inner), F32)
    for h in range(heads):
        steps = jnp.where(head_ids == h, raw[:, h : h + 1], steps)
    steps = jax.nn.softplus(steps + spread(step_bias))
    decays = jnp.exp(-jnp.exp(spread(decay_log)) * steps)

    def turn(target, value):
        target[:, seqs:] = jnp.zeros((inner, LANES - seqs), F32)
        target[:, :seqs] = value.T

    turn(columns_out, steps * inputs)
    turn(decays_out, decays)
    turn(skips_out, spread(skip_gain) * inputs)
    turn(gates_out, gate * jax.nn.sigmoid(gate))
    group = me // readers
    for slot in range(2 * per_group):
        origin = (slot // per_group) * half + group * per_group + slot % per_group

        @pl.when(origin != me)
        def _():
            pltpu.make_async_remote_copy(
                src_ref=mapped,
                dst_ref=arrived.at[slot],
                send_sem=map_send.at[0],
                recv_sem=map_recv.at[slot],
                device_id={"wide": me},
                device_id_type=MESH,
            ).wait_recv()

    out_out[...] = jnp.zeros_like(out_out)
    for slot in range(per_group):
        part = slice(slot * cols, (slot + 1) * cols)
        in_out[:, part] = arrived[slot].astype(F32)
        out_out[part, :seqs] = arrived[per_group + slot].astype(F32).T
    load_state.wait()
    for r in range(readers):
        peer, copy = send(r)

        @pl.when(peer != me)
        def _():
            copy.wait_send()


def state_kernel(
    rows, state, columns, decays, skips, gates, in_maps, out_maps, new_state, gated, total
):
    step = pl.program_id(0)
    heads = state.shape[1]
    inner, seqs = gated.shape
    first = step * rows
    back = lax.rem(LANES - first, LANES)
    lane = lax.broadcasted_iota(jnp.int32, (STATE, LANES), 1)

    @pl.when(step == 0)
    def _():
        total[...] = jnp.zeros_like(total)

    drive = pltpu.roll(columns[...], back, 1)
    fade = [pltpu.roll(decays[h * HEAD_DIM : h * HEAD_DIM + 8, :], back, 1) for h in range(heads)]
    batch = 4
    found = total[...]
    for start in range(0, rows, batch):
        left, right = [], []
        for j in range(start, start + batch):
            maps = in_maps[pl.ds(first + j, 1), :]
            parts = []
            for h in range(heads):
                slow = jnp.broadcast_to(fade[h][:, j : j + 1], (8, LANES))
                for p in range(0, HEAD_DIM, 8):
                    at = h * HEAD_DIM + p
                    fresh = slow * state[first + j, h, p : p + 8] + drive[at : at + 8, j : j + 1] * maps
                    new_state[j, h, p : p + 8] = fresh
                    parts.append(fresh)
            left.append(jnp.concatenate(parts, axis=0).astype(BF16))
            right.append(jnp.where(lane == first + j, out_maps[...], 0.0).astype(BF16))
        found = found + jnp.dot(
            jnp.concatenate(left, axis=1),
            jnp.concatenate(right, axis=0),
            preferred_element_type=F32,
        )
    total[...] = found

    @pl.when(step == pl.num_programs(0) - 1)
    def _():
        gated[...] = ((total[...] + skips[...]) * gates[...])[:, :seqs]


def gather_old(n, me, own, landing, send_sems, recv_sems, meanwhile=None):
    lines, line, side, core = place_of(n, me)
    across = index_of(line, 1 - side, core)
    partner = index_of(line, side, 1 - core)
    sent = []

    def send(src, origin, peer):
        copy = pltpu.make_async_remote_copy(
            src_ref=src,
            dst_ref=landing.at[origin],
            send_sem=send_sems.at[len(sent)],
            recv_sem=recv_sems.at[origin],
            device_id={"wide": peer},
            device_id_type=MESH,
        )
        copy.start()
        sent.append(copy)

    def arrive(origin):
        pltpu.make_async_remote_copy(
            src_ref=own,
            dst_ref=landing.at[origin],
            send_sem=send_sems.at[0],
            recv_sem=recv_sems.at[origin],
            device_id={"wide": partner},
            device_id_type=MESH,
        ).wait_recv()

    for k in range(1, lines):
        send(own, me, index_of(lax.rem(line + k, lines), side, core))
    send(own, me, across)
    send(own, me, partner)
    landing[me] = own[...]
    if meanwhile is not None:
        meanwhile()
    for k in range(1, lines):
        origin = index_of(lax.rem(line + lines - k, lines), side, core)
        arrive(origin)
        send(landing.at[origin], origin, across)
        send(landing.at[origin], origin, partner)
    for k in range(lines):
        origin = index_of(lax.rem(line + lines - k, lines), 1 - side, core)
        arrive(origin)
        send(landing.at[origin], origin, partner)
    for k in range(lines):
        for other in range(2):
            arrive(index_of(lax.rem(line + lines - k, lines), other, 1 - core))
    for copy in sent:
        copy.wait_send()


def expert_kernel(
    n,
    partners,
    gated,
    gated_gain,
    proj_out,
    tokens,
    moe_gain,
    router,
    expert_ids,
    up_hbm,
    down_hbm,
    result,
    up,
    down,
    terms,
    gains,
    router_hi,
    router_lo,
    packing,
    own,
    outgoing,
    hidden_own,
    hidden_all,
    squares,
    squares_in,
    load_sems,
    square_send,
    square_recv,
    hid_send,
    hid_recv,
    *bufs,
):
    me = lax.axis_index("wide")
    width, seqs = tokens.shape
    load_up = pltpu.make_async_copy(up_hbm, up, load_sems.at[0])
    load_down = pltpu.make_async_copy(down_hbm, down, load_sems.at[1])
    load_up.start()
    load_down.start()
    greet_all(n, me)
    values = gated[...].T
    own_squares = jnp.sum(values * values, axis=1, keepdims=True)
    squares[...] = jnp.broadcast_to(own_squares, squares.shape)
    packing[...] = jnp.zeros_like(packing)
    own[...] = jnp.zeros_like(own)
    terms[:width, :] = tokens[...].astype(F32)
    pack_into(own, terms.at[:width, :])
    await_all(n)
    first = (me // partners) * partners
    place = lax.rem(me, partners)

    def partner_copy(k):
        other = lax.rem(place + k, partners)
        return pltpu.make_async_remote_copy(
            src_ref=squares,
            dst_ref=squares_in.at[k - 1],
            send_sem=square_send.at[k - 1],
            recv_sem=square_recv.at[k - 1],
            device_id={"wide": first + other},
            device_id_type=MESH,
        )

    for k in range(1, partners):
        partner_copy(k).start()
    weighted = (values * gated_gain[...].astype(F32)[None]).astype(BF16)
    mixed = jnp.dot(weighted, proj_out[...], preferred_element_type=F32)
    total = own_squares
    for k in range(1, partners):
        partner_copy(k).wait()
        total = total + squares_in[k - 1][:, :1]
    channels = values.shape[1] * partners
    terms[...] = (mixed * lax.rsqrt(total / channels + EPSILON)).T
    for i in range(n):
        pack_into(packing.at[i], terms.at[i * width : (i + 1) * width, :])
        outgoing[i] = packing[i].astype(BF16)

    def prepare():
        gain = moe_gain[...].astype(F32)[None]
        gains[...] = jnp.broadcast_to(gain, (seqs, gain.shape[1])).T
        folded = router[...].astype(F32) * gain
        high = folded.astype(BF16)
        router_hi[...] = high
        router_lo[...] = (folded - high.astype(F32)).astype(BF16)

    half = len(bufs) // 2
    reduced = reduce_all(n, me, outgoing, bufs[:half], prepare)
    hidden_own[...] = (own[...] + reduced).astype(BF16)
    gather_old(n, me, hidden_own, hidden_all, hid_send, hid_recv)
    for i in range(n):
        unpack_into(terms.at[i * width : (i + 1) * width, :], hidden_all[i].astype(F32))
    values = terms[...]
    mean = jnp.mean(values * values, axis=0, keepdims=True)
    moe_scale = lax.rsqrt(mean + EPSILON)
    rounded = values.astype(BF16)
    moe_input = (values * moe_scale * gains[...]).astype(BF16)
    load_up.wait()
    units = jnp.dot(up[0], moe_input, preferred_element_type=F32)
    logits = moe_scale * (
        jnp.dot(router_hi[...], rounded, preferred_element_type=F32)
        + jnp.dot(router_lo[...], rounded, preferred_element_type=F32)
    )
    expert = lax.broadcasted_iota(jnp.int32, logits.shape, 0)
    named = jnp.zeros(logits.shape, F32)
    for k in range(expert_ids.shape[0]):
        named = named + jnp.where(expert == expert_ids[k : k + 1, :], 1.0, 0.0)
    score = named * jax.nn.sigmoid(logits)
    mine = jnp.sum(jnp.where(expert == me, score, 0.0), axis=0, keepdims=True)
    weight = mine / jnp.sum(score, axis=0, keepdims=True)
    active = jnp.square(jnp.maximum(units, 0.0)).T.astype(BF16)
    load_down.wait()
    served = jnp.dot(active, down[0], preferred_element_type=F32)
    terms[...] = served.T.astype(BF16).astype(F32) * weight
    for i in range(n):
        pack_into(packing.at[i], terms.at[i * width : (i + 1) * width, :])
        outgoing[i] = packing[i].astype(BF16)
    reduced = reduce_all(n, me, outgoing, bufs[half:])
    unpack_into(terms.at[:width, :], hidden_own[...].astype(F32) + reduced)
    result[...] = terms[:width, :].astype(BF16)


def vmem(count):
    return [pl.BlockSpec(memory_space=pltpu.VMEM)] * count


ANY = pl.BlockSpec(memory_space=pltpu.HBM)
DMA = pltpu.SemaphoreType.DMA


def local(
    n,
    tokens,
    mix_gain,
    proj_inner,
    proj_maps,
    proj_step,
    window_inner,
    window_maps,
    kernel_inner,
    kernel_maps,
    step_bias,
    decay_log,
    skip_gain,
    gated_gain,
    proj_out,
    ssm_state,
    moe_gain,
    router_weight,
    expert_ids,
    expert_up,
    expert_down,
):
    seqs, width = tokens.shape
    full_width = proj_inner.shape[0]
    inner = proj_inner.shape[2]
    cols = proj_maps.shape[1]
    heads = proj_step.shape[1]
    readers = HEADS // GROUPS // heads
    slots = 2 * (STATE // cols)
    kept = packed_shape(width, seqs)[0]
    first, last = extra_rows(width, seqs)
    across = 2 * LANES + 2 * inner
    scalars = pl.BlockSpec(memory_space=pltpu.SMEM)
    state, columns, decays, skips, gates, in_maps, out_maps = pl.pallas_call(
        functools.partial(gather_kernel, n),
        out_shape=(
            pltpu.VMEM(ssm_state.shape, F32),
            pltpu.VMEM((inner, LANES), F32),
            pltpu.VMEM((inner, LANES), F32),
            pltpu.VMEM((inner, LANES), F32),
            pltpu.VMEM((inner, LANES), F32),
            pltpu.VMEM((seqs, STATE), F32),
            pltpu.VMEM((STATE, LANES), F32),
        ),
        in_specs=vmem(2) + [ANY] * 2 + vmem(5) + [scalars] * 3 + [ANY],
        out_specs=tuple(vmem(7)),
        scratch_shapes=[
            pltpu.VMEM((n, kept, LANES), BF16),
            pltpu.VMEM((kept, LANES), BF16),
            pltpu.VMEM((full_width, 2, inner), BF16),
            pltpu.VMEM((full_width, cols), BF16),
            pltpu.VMEM((n, width, across), BF16),
            pltpu.VMEM((seqs, across), F32),
            pltpu.VMEM((last - first, LANES), F32),
            pltpu.VMEM((seqs, cols), BF16),
            pltpu.VMEM((slots, seqs, cols), BF16),
            DMA((3,)),
            DMA((n,)),
            DMA((n,)),
            DMA((readers,)),
            DMA((slots,)),
        ],
        compiler_params=pltpu.CompilerParams(
            collective_id=0, has_side_effects=True, vmem_limit_bytes=51 << 20
        ),
        name="gather_tokens",
    )(
        tokens.T,
        mix_gain,
        proj_inner,
        proj_maps,
        proj_step.T,
        window_inner.transpose(1, 0, 2),
        window_maps.transpose(1, 0, 2),
        kernel_inner,
        kernel_maps,
        step_bias,
        decay_log,
        skip_gain,
        ssm_state,
    )
    rows = 16
    new_state, gated = pl.pallas_call(
        functools.partial(state_kernel, rows),
        grid=(seqs // rows,),
        out_shape=(
            jax.ShapeDtypeStruct(ssm_state.shape, F32),
            pltpu.VMEM((inner, seqs), F32),
        ),
        in_specs=vmem(7),
        out_specs=(
            pl.BlockSpec((rows, heads, HEAD_DIM, STATE), lambda i: (i, 0, 0, 0)),
            vmem(1)[0],
        ),
        scratch_shapes=[pltpu.VMEM((inner, LANES), F32)],
        compiler_params=pltpu.CompilerParams(vmem_limit_bytes=16 << 20),
        name="update_state",
    )(state, columns, decays, skips, gates, in_maps, out_maps)
    lines = n // 4

    def piece(count):
        return pltpu.VMEM((count, kept, LANES), BF16)

    reduce_bufs = [
        piece(2 * lines),
        piece(lines),
        piece(lines),
        piece(lines),
        piece(lines),
        DMA((4 * lines - 1,)),
        DMA((2 * lines,)),
        DMA((lines,)),
        DMA((lines,)),
    ]
    up_shape = (1, expert_up.shape[2], full_width)
    next_hidden = pl.pallas_call(
        functools.partial(expert_kernel, n, readers),
        out_shape=jax.ShapeDtypeStruct((width, seqs), BF16),
        in_specs=vmem(7) + [ANY, ANY],
        out_specs=vmem(1)[0],
        scratch_shapes=[
            pltpu.VMEM(up_shape, BF16),
            pltpu.VMEM(expert_down.shape, BF16),
            pltpu.VMEM((full_width, seqs), F32),
            pltpu.VMEM((full_width, seqs), F32),
            pltpu.VMEM((router_weight.shape[1], full_width), BF16),
            pltpu.VMEM((router_weight.shape[1], full_width), BF16),
            pltpu.VMEM((n, kept, LANES), F32),
            pltpu.VMEM((kept, LANES), F32),
            piece(n),
            pltpu.VMEM((kept, LANES), BF16),
            piece(n),
            pltpu.VMEM((seqs, 128), F32),
            pltpu.VMEM((readers - 1, seqs, 128), F32),
            DMA((2,)),
            DMA((readers - 1,)),
            DMA((readers - 1,)),
            DMA((n,)),
            DMA((n,)),
        ]
        + reduce_bufs * 2,
        compiler_params=pltpu.CompilerParams(
            collective_id=1, has_side_effects=True, vmem_limit_bytes=46 << 20
        ),
        name="mix_and_serve",
    )(
        gated,
        gated_gain,
        proj_out,
        tokens.T,
        moe_gain,
        router_weight.T,
        expert_ids.T,
        expert_up.swapaxes(1, 2),
        expert_down,
    )
    return (next_hidden.T, new_state)


def solution(mesh):
    in_specs = (
        P("group", "wide"),
        P(),
        P(None, None, "wide"),
        P(None, "wide"),
        P(None, "wide"),
        P("group", None, "wide"),
        P("group", None, "wide"),
        P(None, "wide"),
        P(None, "wide"),
        P("wide"),
        P("wide"),
        P("wide"),
        P("wide"),
        P("wide", None),
        P("group", "wide", None, None),
        P(),
        P(),
        P("group", None),
        P("wide", None, None),
        P("wide", None, None),
    )
    out_specs = (P("group", "wide"), P("group", "wide", None, None))
    body = functools.partial(local, mesh.shape["wide"])
    return jax.shard_map(body, mesh=mesh, in_specs=in_specs, out_specs=out_specs, check_vma=False)
```

time: 83 us -> 72.6 us (0.87)
  Pallas kernels: 77 us -> 68.6 us
  matrix products: 1.21 us -> 0 us
    pallas_call x2, Pallas kernels: 34.7 us -> 28 us  [the longest x1 20 us: local(): pl.pallas_call(functools.partial(gather_kernel, n), out_shape=(pltpu.VMEM...]
    pallas_call x1, Pallas kernels: 42.3 us -> 40.6 us  [local(): pl.pallas_call(functools.partial(expert_kernel, n, readers), out_shape=ja...]
    dot_general x1 -> x0, matrix products: 1.21 us -> none  [local(): jnp.dot(normed, proj_inner.reshape(full_width, 2 * inner), preferred_elem...]
    unnamed x4 -> x15, local copies, waits for them, and re-layouts: 3.7 us -> 3.07 us
where the time goes in v1:
time: 72.6 us; the launch traced here: 72.4 us
  Pallas kernels  68.6 us (94%)
  local copies, waits for them, and re-layouts  3.07 us (4%)
  between operations  0.74 us (1%)
    pallas_call x1, Pallas kernels, local(): pl.pallas_call(functools.partial(expert_kernel, n, readers), out_shape=ja...  40.6 us
    pallas_call x1, Pallas kernels, local(): pl.pallas_call(functools.partial(gather_kernel, n), out_shape=(pltpu.VMEM...  20 us
    pallas_call x1, Pallas kernels, local(): pl.pallas_call(functools.partial(state_kernel, rows), grid=(seqs // rows,...  7.93 us
    unnamed x15, local copies, waits for them, and re-layouts  3.07 us

profile of v1, /device:TPU:0, one launch (start us, length us, event | category | flops | bytes accessed | tf_op | source)
XLA Modules:
  0.0 72.4 jit_solution(13723409429280407975)
XLA Ops:
  0.6 20.0 %gather_tokens.1 = (f32[96,4,64,128]{3,2,1,0:T(8,128)S(1)}, f32[256,128]{1,0:T(8,128)S(1)}, f32[256,128]{1,0:T(8,128)S(1)}, f32[256,128]{1,0:T(8,128)S(1)}, f32[...) custom-call(bf16[168,96]{1,0:T(8,128)(2,1)} %bitcast.9, bf16[2688]{0:T(1024)(128)(2,1)} %gain.1, ...), custom_call_target="tpu_custom_call" | custom-call | tf_op jit(solution)/shard_map/gather_tokens/pallas_call | solution.py:708
  20.7 0.0 copy-start.1
  20.7 0.0 copy-start.2
  20.7 0.0 copy-start.3
  20.7 0.0 copy-start.4
  20.7 0.0 copy-start.5
  20.7 0.0 copy-start.6
  20.7 7.9 %update_state.1 = (f32[96,4,64,128]{3,2,1,0:T(8,128)}, f32[256,96]{1,0:T(8,128)S(1)}) custom-call(f32[96,4,64,128]{3,2,1,0:T(8,128)S(1)} %get-tuple-element.11.state, f32[256,128]{1,0:T(8,128)S(1)} %get-tuple-element.12.columns, f32[256,128]{1,0:T(8,128)S(1)} %get-tuple-element.13.decays, f32[256,128]{1,0:T(8,128)S(1)} %get-tuple-element.14.skips, ...), custom_call_target="tpu_custom_call" | custom-call | tf_op jit(solution)/shard_map/update_state/pallas_call | solution.py:757
  28.7 0.0 copy-done.1
  28.7 0.0 copy-done.2
  28.7 0.0 copy-done.3
  28.7 0.0 copy-done.4
  28.7 0.0 copy-done.5
  28.7 0.0 copy-done.6
  28.7 0.0 copy-start
  28.7 2.4 %copy-done = bf16[1,2688,928]{1,2,0:T(8,128)(2,1)S(1)} copy-done((bf16[1,2688,928]{1,2,0:T(8,128)(2,1)S(1)}, bf16[1,2688,928]{1,2,0:T(8,128)(2,1)}, u32[]{:S(2)}) %copy-start) | copy-done | bytes 4988952
  31.1 40.6 %mix_and_serve.1 = bf16[168,96]{1,0:T(8,128)(2,1)S(1)} custom-call(f32[256,96]{1,0:T(8,128)S(1)} %get-tuple-element.18.gated, bf16[256]{0:T(256)(128)(2,1)S(1)} %copy-done.6, bf16[256,2688]{1,0:T(8,128)(2,1)S(1)} %copy-done.1, bf16[168,96]{1,0:T(8,128)(2,1)S(1)} %bitcast.10, bf16[2688]{0:T(1024)(128)(2,1)S(1)} %copy-done.4, bf16[16,2688]{1,0:T(8,128)(2,1)S(1)} %bitcast.12, ...), custom_call_target="tpu_custom_call" | custom-call | tf_op jit(solution)/shard_map/mix_and_serve/pallas_call | solution.py:790
  71.8 0.6 copy.23
Async XLA Ops:
  20.7 8.0 %copy-start.1 = (bf16[256,2688]{1,0:T(8,128)(2,1)S(1)}, bf16[256,2688]{1,0:T(8,128)(2,1)}, u32[]{:S(2)}) copy-start(bf16[256,2688]{1,0:T(8,128)(2,1)} %proj_out.1) | copy-start | bytes 4128772
  20.7 8.0 %copy-start.2 = (bf16[96,168]{0,1:T(8,128)(2,1)S(1)}, bf16[96,168]{0,1:T(8,128)(2,1)}, u32[]{:S(2)}) copy-start(bf16[96,168]{0,1:T(8,128)(2,1)} %param.20) | copy-start | bytes 96772
  20.7 8.0 %copy-start.3 = (bf16[2688,16]{0,1:T(8,128)(2,1)S(1)}, bf16[2688,16]{0,1:T(8,128)(2,1)}, u32[]{:S(2)}) copy-start(bf16[2688,16]{0,1:T(8,128)(2,1)} %param.36) | copy-start | bytes 258052
  20.7 8.0 %copy-start.4 = (bf16[2688]{0:T(1024)(128)(2,1)S(1)}, bf16[2688]{0:T(1024)(128)(2,1)}, u32[]{:S(2)}) copy-start(bf16[2688]{0:T(1024)(128)(2,1)} %moe_gain.1) | copy-start | bytes 16132
  20.7 8.0 %copy-start.5 = (s32[96,6]{0,1:T(8,128)S(1)}, s32[96,6]{0,1:T(8,128)}, u32[]{:S(2)}) copy-start(s32[96,6]{0,1:T(8,128)} %param.37) | copy-start | bytes 6916
  20.7 8.0 %copy-start.6 = (bf16[256]{0:T(256)(128)(2,1)S(1)}, bf16[256]{0:T(256)(128)(2,1)}, u32[]{:S(2)}) copy-start(bf16[256]{0:T(256)(128)(2,1)} %gated_gain.1) | copy-start | bytes 1540
  28.7 2.4 %copy-start = (bf16[1,2688,928]{1,2,0:T(8,128)(2,1)S(1)}, bf16[1,2688,928]{1,2,0:T(8,128)(2,1)}, u32[]{:S(2)}) copy-start(bf16[1,2688,928]{1,2,0:T(8,128)(2,1)} %param.38) | copy-start | bytes 14966788

commit v2 on v1

--- a/solution.py
+++ b/solution.py
@@ -101,8 +101,8 @@
         copy.wait_send()
 
 
-def reduce_all(n, me, blocks, bufs, meanwhile=None):
-    core_in, side_out, side_in, line_out, line_in, sends, core_sem, side_sem, line_sem = bufs
+def reduce_all(n, me, make, enter, bufs, finish, early, late):
+    outgoing, mine, core_in, side_out, side_in, line_out, line_in, sends, core_sem, side_sem, line_sem = bufs
     lines, line, side, core = place_of(n, me)
     across = index_of(line, 1 - side, core)
     partner = index_of(line, side, 1 - core)
@@ -129,53 +129,47 @@
     def ahead(k):
         return lax.rem(line + k, lines)
 
+    order = [(k, other) for k in range(1, lines + 1) for other in (1 - side, side)]
+    if enter is not None:
+        for number, (k, other) in enumerate(order):
+            outgoing[number] = make(index_of(ahead(k), other, 1 - core)).astype(BF16)
+        enter()
+    for number, (k, other) in enumerate(order):
+        if enter is None:
+            outgoing[number] = make(index_of(ahead(k), other, 1 - core)).astype(BF16)
+        send(outgoing.at[number], core_in.at[number], core_sem.at[number], partner)
+    for number, (k, other) in enumerate(order):
+        mine[number] = make(index_of(ahead(k), other, core))
+
+    def pair_sum(number):
+        arrive(core_in.at[number], core_sem.at[number])
+        return finish(mine[number] + core_in[number].astype(F32))
+
     for k in range(1, lines + 1):
-        for turn in range(2):
-            other = 1 - side if turn == 0 else side
-            slot = ahead(k) * 2 + other
-            send(
-                blocks.at[index_of(ahead(k), other, 1 - core)],
-                core_in.at[slot],
-                core_sem.at[slot],
-                partner,
-            )
-
-    def pair_sum(k, other):
-        slot = ahead(k) * 2 + other
-        arrive(core_in.at[slot], core_sem.at[slot])
-        return blocks[index_of(ahead(k), other, core)].astype(F32) + core_in[slot].astype(F32)
-
-    def second(k):
-        slot = ahead(k)
-        side_out[slot] = pair_sum(k, 1 - side).astype(BF16)
+        slot = k - 1
+        side_out[slot] = pair_sum(2 * slot).astype(BF16)
         send(side_out.at[slot], side_in.at[slot], side_sem.at[slot], across)
+    early()
 
     def third(k):
-        slot = ahead(k)
-        value = pair_sum(k, side)
+        slot = k - 1
+        value = pair_sum(2 * slot + 1)
         arrive(side_in.at[slot], side_sem.at[slot])
-        value = value + side_in[slot].astype(F32)
-        if k == lines:
-            return value
-        line_out[slot] = value.astype(BF16)
+        return value + side_in[slot].astype(F32)
+
+    for k in range(1, lines):
+        line_out[k - 1] = third(k).astype(BF16)
         send(
-            line_out.at[slot],
-            line_in.at[line],
-            line_sem.at[line],
-            index_of(slot, side, core),
+            line_out.at[k - 1],
+            line_in.at[k - 1],
+            line_sem.at[k - 1],
+            index_of(ahead(k), side, core),
         )
-
-    second(1)
+    total = third(lines)
+    late()
     for k in range(1, lines):
-        second(k + 1)
-        third(k)
-    if meanwhile is not None:
-        meanwhile()
-    total = third(lines)
-    for k in range(1, lines):
-        slot = lax.rem(line + lines - k, lines)
-        arrive(line_in.at[slot], line_sem.at[slot])
-        total = total + line_in[slot].astype(F32)
+        arrive(line_in.at[k - 1], line_sem.at[k - 1])
+        total = total + line_in[k - 1].astype(F32)
     for copy in sent:
         copy.wait_send()
     return total
@@ -191,24 +185,6 @@
     chunks = seqs // gap
     rest = width // (chunks + 1) // 8 * 8
     return width - rest, rest, gap
-
-
-def pack_into(target, source):
-    width, seqs = source.shape
-    kept, rest, gap = packed_shape(width, seqs)
-    target[:, :seqs] = source[:kept, :]
-    if rest:
-        for c in range(seqs // gap):
-            target[c * rest : (c + 1) * rest, seqs:] = source[kept:, c * gap : (c + 1) * gap]
-
-
-def unpack_into(target, value):
-    width, seqs = target.shape
-    kept, rest, gap = packed_shape(width, seqs)
-    target[:kept, :] = value[:, :seqs]
-    if rest:
-        for c in range(seqs // gap):
-            target[kept:, c * gap : (c + 1) * gap] = value[c * rest : (c + 1) * rest, seqs:]
 
 
 def lane_ids(rows):
@@ -253,6 +229,23 @@
 def padded(value):
     rows, lanes = value.shape
     return jnp.concatenate([value, jnp.zeros((rows, LANES - lanes), F32)], axis=1)
+
+
+def by_block(target, value, start, width, columns):
+    at, count = 0, value.shape[0]
+    while at < count:
+        block, row = divmod(start + at, width)
+        size = min(width - row, count - at)
+        target[block, row : row + size, :columns] = value[at : at + size]
+        at += size
+
+
+def token_scale(squares, seqs, channels):
+    rows = squares.shape[0]
+    chunks = rows // 2
+    turned = jnp.concatenate([squares[...], jnp.zeros((LANES - rows, LANES), F32)], axis=0).T
+    pieces = [turned[seqs:, c : c + 1] + turned[seqs:, chunks + c : chunks + c + 1] for c in range(chunks)]
+    return lax.rsqrt(jnp.concatenate(pieces, axis=0) / channels + EPSILON)
 
 
 def halves(value):
@@ -282,6 +275,8 @@
     decay_log,
     skip_gain,
     state_hbm,
+    proj_hbm,
+    gated_gain,
     state,
     columns_out,
     decays_out,
@@ -289,10 +284,13 @@
     gates_out,
     in_out,
     out_out,
+    gains_out,
+    proj_turned,
     landing,
     own,
     raw_inner,
     raw_maps,
+    raw_proj,
     weights,
     total,
     squares,
@@ -312,8 +310,10 @@
     load_inner = pltpu.make_async_copy(inner_hbm, raw_inner, load_sems.at[0])
     load_maps = pltpu.make_async_copy(maps_hbm, raw_maps, load_sems.at[1])
     load_state = pltpu.make_async_copy(state_hbm, state, load_sems.at[2])
+    load_proj = pltpu.make_async_copy(proj_hbm, raw_proj, load_sems.at[3])
     load_inner.start()
     load_maps.start()
+    load_proj.start()
     load_state.start()
     greet_all(n, me)
     values = padded(tokens[...].astype(F32))
@@ -341,6 +341,10 @@
             for j in range(2):
                 at = LANES * 2 + j * inner
                 weights[i, :, at : at + inner] = split[j * width : (j + 1) * width]
+        gains_out[...] = jnp.broadcast_to(gated_gain[...].astype(F32)[None], (LANES, inner)).T
+        load_proj.wait()
+        for start in range(0, n * width, LANES):
+            by_block(proj_turned, raw_proj[:, start : start + LANES].T, start, width, inner)
 
     def consume(block, origin):
         value = block[...].astype(F32)
@@ -352,14 +356,7 @@
 
     await_all(n)
     gather_all(n, me, own, landing, send_sems, recv_sems, consume, prepare)
-    chunks = (last - first) // 2
-    gap = seqs // chunks
-    turned = jnp.concatenate([squares[...], jnp.zeros((LANES - last + first, LANES), F32)], axis=0).T
-    pieces = [
-        turned[seqs:, c : c + 1] + turned[seqs:, chunks + c : chunks + c + 1] for c in range(chunks)
-    ]
-    mean = jnp.concatenate(pieces, axis=0) / (n * width)
-    scale = lax.rsqrt(mean + EPSILON)
+    scale = token_scale(squares, seqs, n * width)
 
     def projected(at, count):
         return (total[:, at : at + count] * scale).astype(BF16).astype(F32)
@@ -449,11 +446,10 @@
 
 
 def state_kernel(
-    rows, state, columns, decays, skips, gates, in_maps, out_maps, new_state, gated, total
+    rows, seqs, state, columns, decays, skips, gates, in_maps, out_maps, gains, new_state, weighted, sums, total
 ):
     step = pl.program_id(0)
     heads = state.shape[1]
-    inner, seqs = gated.shape
     first = step * rows
     back = lax.rem(LANES - first, LANES)
     lane = lax.broadcasted_iota(jnp.int32, (STATE, LANES), 1)
@@ -489,66 +485,17 @@
 
     @pl.when(step == pl.num_programs(0) - 1)
     def _():
-        gated[...] = ((total[...] + skips[...]) * gates[...])[:, :seqs]
-
-
-def gather_old(n, me, own, landing, send_sems, recv_sems, meanwhile=None):
-    lines, line, side, core = place_of(n, me)
-    across = index_of(line, 1 - side, core)
-    partner = index_of(line, side, 1 - core)
-    sent = []
-
-    def send(src, origin, peer):
-        copy = pltpu.make_async_remote_copy(
-            src_ref=src,
-            dst_ref=landing.at[origin],
-            send_sem=send_sems.at[len(sent)],
-            recv_sem=recv_sems.at[origin],
-            device_id={"wide": peer},
-            device_id_type=MESH,
-        )
-        copy.start()
-        sent.append(copy)
-
-    def arrive(origin):
-        pltpu.make_async_remote_copy(
-            src_ref=own,
-            dst_ref=landing.at[origin],
-            send_sem=send_sems.at[0],
-            recv_sem=recv_sems.at[origin],
-            device_id={"wide": partner},
-            device_id_type=MESH,
-        ).wait_recv()
-
-    for k in range(1, lines):
-        send(own, me, index_of(lax.rem(line + k, lines), side, core))
-    send(own, me, across)
-    send(own, me, partner)
-    landing[me] = own[...]
-    if meanwhile is not None:
-        meanwhile()
-    for k in range(1, lines):
-        origin = index_of(lax.rem(line + lines - k, lines), side, core)
-        arrive(origin)
-        send(landing.at[origin], origin, across)
-        send(landing.at[origin], origin, partner)
-    for k in range(lines):
-        origin = index_of(lax.rem(line + lines - k, lines), 1 - side, core)
-        arrive(origin)
-        send(landing.at[origin], origin, partner)
-    for k in range(lines):
-        for other in range(2):
-            arrive(index_of(lax.rem(line + lines - k, lines), other, 1 - core))
-    for copy in sent:
-        copy.wait_send()
+        gated = (total[...] + skips[...]) * gates[...]
+        sums[...] = jnp.broadcast_to(jnp.sum(gated * gated, axis=0, keepdims=True), sums.shape)
+        weighted[...] = (gated * gains[...]).astype(BF16)
 
 
 def expert_kernel(
     n,
     partners,
-    gated,
-    gated_gain,
-    proj_out,
+    weighted,
+    sums,
+    proj_turned,
     tokens,
     moe_gain,
     router,
@@ -558,109 +505,134 @@
     result,
     up,
     down,
-    terms,
+    up_turned,
+    down_turned,
+    own,
+    landing,
+    total,
+    squares,
     gains,
-    router_hi,
-    router_lo,
-    packing,
-    own,
-    outgoing,
-    hidden_own,
-    hidden_all,
-    squares,
-    squares_in,
+    sums_in,
     load_sems,
-    square_send,
-    square_recv,
+    sum_send,
+    sum_recv,
     hid_send,
     hid_recv,
     *bufs,
 ):
     me = lax.axis_index("wide")
     width, seqs = tokens.shape
+    hidden_units = up.shape[1]
+    experts = router.shape[0]
+    extent = up_turned.shape[2]
+    kept, rest, gap = packed_shape(width, seqs)
+    chunks = seqs // gap
     load_up = pltpu.make_async_copy(up_hbm, up, load_sems.at[0])
     load_down = pltpu.make_async_copy(down_hbm, down, load_sems.at[1])
     load_up.start()
     load_down.start()
     greet_all(n, me)
-    values = gated[...].T
-    own_squares = jnp.sum(values * values, axis=1, keepdims=True)
-    squares[...] = jnp.broadcast_to(own_squares, squares.shape)
-    packing[...] = jnp.zeros_like(packing)
-    own[...] = jnp.zeros_like(own)
-    terms[:width, :] = tokens[...].astype(F32)
-    pack_into(own, terms.at[:width, :])
-    await_all(n)
     first = (me // partners) * partners
     place = lax.rem(me, partners)
 
     def partner_copy(k):
         other = lax.rem(place + k, partners)
         return pltpu.make_async_remote_copy(
-            src_ref=squares,
-            dst_ref=squares_in.at[k - 1],
-            send_sem=square_send.at[k - 1],
-            recv_sem=square_recv.at[k - 1],
+            src_ref=sums,
+            dst_ref=sums_in.at[k - 1],
+            send_sem=sum_send.at[k - 1],
+            recv_sem=sum_recv.at[k - 1],
             device_id={"wide": first + other},
             device_id_type=MESH,
         )
 
-    for k in range(1, partners):
-        partner_copy(k).start()
-    weighted = (values * gated_gain[...].astype(F32)[None]).astype(BF16)
-    mixed = jnp.dot(weighted, proj_out[...], preferred_element_type=F32)
-    total = own_squares
-    for k in range(1, partners):
-        partner_copy(k).wait()
-        total = total + squares_in[k - 1][:, :1]
-    channels = values.shape[1] * partners
-    terms[...] = (mixed * lax.rsqrt(total / channels + EPSILON)).T
-    for i in range(n):
-        pack_into(packing.at[i], terms.at[i * width : (i + 1) * width, :])
-        outgoing[i] = packing[i].astype(BF16)
-
-    def prepare():
-        gain = moe_gain[...].astype(F32)[None]
-        gains[...] = jnp.broadcast_to(gain, (seqs, gain.shape[1])).T
-        folded = router[...].astype(F32) * gain
-        high = folded.astype(BF16)
-        router_hi[...] = high
-        router_lo[...] = (folded - high.astype(F32)).astype(BF16)
+    def mixed(i):
+        return pack(jnp.dot(proj_turned[i], weighted[...], preferred_element_type=F32), seqs)
+
+    def enter():
+        await_all(n)
+        for k in range(1, partners):
+            partner_copy(k).start()
+
+    scales = []
+
+    def scaled(value):
+        if not scales:
+            whole = sums[...]
+            for k in range(1, partners):
+                partner_copy(k).wait()
+                whole = whole + sums_in[k - 1]
+            row = lax.rsqrt(whole[:1] / (weighted.shape[0] * partners) + EPSILON)
+            scales.append(pack(jnp.broadcast_to(row, (width, LANES)), seqs))
+        return value * scales[0]
+
+    def turn_up():
+        gains[...] = pack(own_columns(moe_gain, n, me, width), seqs)
+        load_up.wait()
+        for start in range(0, n * width, LANES):
+            lanes = slice(start, start + LANES)
+            spare = jnp.zeros((extent - hidden_units - experts, LANES), BF16)
+            tall = jnp.concatenate([up[0, :, lanes], router[:, lanes], spare], axis=0)
+            by_block(up_turned, tall.T, start, width, extent)
+
+    def turn_down():
+        load_down.wait()
+        for start in range(0, n * width, LANES):
+            by_block(down_turned, down[0, :, start : start + LANES].T, start, width, hidden_units)
+
+    def nothing():
+        pass
 
     half = len(bufs) // 2
-    reduced = reduce_all(n, me, outgoing, bufs[:half], prepare)
-    hidden_own[...] = (own[...] + reduced).astype(BF16)
-    gather_old(n, me, hidden_own, hidden_all, hid_send, hid_recv)
-    for i in range(n):
-        unpack_into(terms.at[i * width : (i + 1) * width, :], hidden_all[i].astype(F32))
-    values = terms[...]
-    mean = jnp.mean(values * values, axis=0, keepdims=True)
-    moe_scale = lax.rsqrt(mean + EPSILON)
-    rounded = values.astype(BF16)
-    moe_input = (values * moe_scale * gains[...]).astype(BF16)
-    load_up.wait()
-    units = jnp.dot(up[0], moe_input, preferred_element_type=F32)
-    logits = moe_scale * (
-        jnp.dot(router_hi[...], rounded, preferred_element_type=F32)
-        + jnp.dot(router_lo[...], rounded, preferred_element_type=F32)
-    )
-    expert = lax.broadcasted_iota(jnp.int32, logits.shape, 0)
-    named = jnp.zeros(logits.shape, F32)
+    reduced = reduce_all(n, me, mixed, enter, bufs[:half], scaled, turn_up, nothing)
+    held = pack(padded(tokens[...].astype(F32)), seqs)
+    held = (held + reduced).astype(BF16).astype(F32)
+    power = held * held
+    main = jnp.sum(power, axis=0, keepdims=True)
+    extra = []
+    for c in range(chunks):
+        tail = jnp.sum(power[c * rest : (c + 1) * rest], axis=0, keepdims=True)
+        extra.append(pltpu.roll(main, seqs - c * gap, 1) + tail)
+    spare = jnp.zeros((kept - rest * chunks - 2 * chunks, LANES), F32)
+    both = [halves(row) for row in extra]
+    ending = jnp.concatenate([row[0] for row in both] + [row[1] for row in both] + [spare], axis=0)
+    sender = held * gains[...]
+    inside = lane_ids(kept - rest * chunks) < seqs
+    ending = jnp.where(inside, sender[rest * chunks :], ending)
+    own[...] = jnp.concatenate([sender[: rest * chunks], ending], axis=0).astype(BF16)
+    total[...] = jnp.zeros_like(total)
+    squares[...] = jnp.zeros_like(squares)
+    begin, end = extra_rows(width, seqs)
+
+    def consume(block, origin):
+        value = block[...].astype(F32)
+        squares[...] += value[begin:end]
+        fresh = unpack(value, width, seqs)[:, :seqs].astype(BF16)
+        total[...] += lax.dot_general(
+            fresh, up_turned[origin], (((0,), (0,)), ((), ())), preferred_element_type=F32
+        )
+
+    gather_all(n, me, own, landing, hid_send, hid_recv, consume, turn_down)
+    scale = token_scale(squares, seqs, n * width)
+    logits = total[:, hidden_units : hidden_units + experts] * scale
+    expert = lax.broadcasted_iota(jnp.int32, (LANES, seqs), 0)
+    named = jnp.zeros((LANES, seqs), F32)
     for k in range(expert_ids.shape[0]):
         named = named + jnp.where(expert == expert_ids[k : k + 1, :], 1.0, 0.0)
-    score = named * jax.nn.sigmoid(logits)
-    mine = jnp.sum(jnp.where(expert == me, score, 0.0), axis=0, keepdims=True)
-    weight = mine / jnp.sum(score, axis=0, keepdims=True)
-    active = jnp.square(jnp.maximum(units, 0.0)).T.astype(BF16)
-    load_down.wait()
-    served = jnp.dot(active, down[0], preferred_element_type=F32)
-    terms[...] = served.T.astype(BF16).astype(F32) * weight
-    for i in range(n):
-        pack_into(packing.at[i], terms.at[i * width : (i + 1) * width, :])
-        outgoing[i] = packing[i].astype(BF16)
-    reduced = reduce_all(n, me, outgoing, bufs[half:])
-    unpack_into(terms.at[:width, :], hidden_own[...].astype(F32) + reduced)
-    result[...] = terms[:width, :].astype(BF16)
+    score = named.T[:, :experts] * jax.nn.sigmoid(logits)
+    lane = lax.broadcasted_iota(jnp.int32, score.shape, 1)
+    mine = jnp.sum(jnp.where(lane == me, score, 0.0), axis=1, keepdims=True)
+    weight = mine / jnp.sum(score, axis=1, keepdims=True)
+    units = jnp.maximum(total[:, :hidden_units] * scale, 0.0)
+    active = jnp.square(units) * weight
+    active = jnp.concatenate([active, jnp.zeros((LANES - seqs, hidden_units), F32)], axis=0)
+    active = active.astype(BF16).T
+
+    def served(i):
+        return pack(jnp.dot(down_turned[i], active, preferred_element_type=F32), seqs)
+
+    reduced = reduce_all(n, me, served, None, bufs[half:], lambda value: value, nothing, nothing)
+    result[...] = unpack(held + reduced, width, seqs)[:, :seqs].astype(BF16)
 
 
 def vmem(count):
@@ -705,7 +677,7 @@
     first, last = extra_rows(width, seqs)
     across = 2 * LANES + 2 * inner
     scalars = pl.BlockSpec(memory_space=pltpu.SMEM)
-    state, columns, decays, skips, gates, in_maps, out_maps = pl.pallas_call(
+    state, columns, decays, skips, gates, in_maps, out_maps, gains, proj_turned = pl.pallas_call(
         functools.partial(gather_kernel, n),
         out_shape=(
             pltpu.VMEM(ssm_state.shape, F32),
@@ -715,27 +687,30 @@
             pltpu.VMEM((inner, LANES), F32),
             pltpu.VMEM((seqs, STATE), F32),
             pltpu.VMEM((STATE, LANES), F32),
+            pltpu.VMEM((inner, LANES), F32),
+            pltpu.VMEM((n, width, inner), BF16),
         ),
-        in_specs=vmem(2) + [ANY] * 2 + vmem(5) + [scalars] * 3 + [ANY],
-        out_specs=tuple(vmem(7)),
+        in_specs=vmem(2) + [ANY] * 2 + vmem(5) + [scalars] * 3 + [ANY] * 2 + vmem(1),
+        out_specs=tuple(vmem(9)),
         scratch_shapes=[
             pltpu.VMEM((n, kept, LANES), BF16),
             pltpu.VMEM((kept, LANES), BF16),
             pltpu.VMEM((full_width, 2, inner), BF16),
             pltpu.VMEM((full_width, cols), BF16),
+            pltpu.VMEM((inner, full_width), BF16),
             pltpu.VMEM((n, width, across), BF16),
             pltpu.VMEM((seqs, across), F32),
             pltpu.VMEM((last - first, LANES), F32),
             pltpu.VMEM((seqs, cols), BF16),
             pltpu.VMEM((slots, seqs, cols), BF16),
-            DMA((3,)),
+            DMA((4,)),
             DMA((n,)),
             DMA((n,)),
             DMA((readers,)),
             DMA((slots,)),
         ],
         compiler_params=pltpu.CompilerParams(
-            collective_id=0, has_side_effects=True, vmem_limit_bytes=51 << 20
+            collective_id=0, has_side_effects=True, vmem_limit_bytes=49 << 20
         ),
         name="gather_tokens",
     )(
@@ -752,30 +727,35 @@
         decay_log,
         skip_gain,
         ssm_state,
+        proj_out,
+        gated_gain,
     )
     rows = 16
-    new_state, gated = pl.pallas_call(
-        functools.partial(state_kernel, rows),
+    new_state, weighted, sums = pl.pallas_call(
+        functools.partial(state_kernel, rows, seqs),
         grid=(seqs // rows,),
         out_shape=(
             jax.ShapeDtypeStruct(ssm_state.shape, F32),
-            pltpu.VMEM((inner, seqs), F32),
+            pltpu.VMEM((inner, LANES), BF16),
+            pltpu.VMEM((8, LANES), F32),
         ),
-        in_specs=vmem(7),
+        in_specs=vmem(8),
         out_specs=(
             pl.BlockSpec((rows, heads, HEAD_DIM, STATE), lambda i: (i, 0, 0, 0)),
-            vmem(1)[0],
+            *vmem(2),
         ),
         scratch_shapes=[pltpu.VMEM((inner, LANES), F32)],
         compiler_params=pltpu.CompilerParams(vmem_limit_bytes=16 << 20),
         name="update_state",
-    )(state, columns, decays, skips, gates, in_maps, out_maps)
+    )(state, columns, decays, skips, gates, in_maps, out_maps, gains)
     lines = n // 4
 
-    def piece(count):
-        return pltpu.VMEM((count, kept, LANES), BF16)
+    def piece(count, kind=BF16):
+        return pltpu.VMEM((count, kept, LANES), kind)
 
     reduce_bufs = [
+        piece(2 * lines),
+        piece(2 * lines, F32),
         piece(2 * lines),
         piece(lines),
         piece(lines),
@@ -786,26 +766,25 @@
         DMA((lines,)),
         DMA((lines,)),
     ]
-    up_shape = (1, expert_up.shape[2], full_width)
+    hidden_units = expert_up.shape[2]
+    experts = router_weight.shape[1]
+    extent = -(-(hidden_units + experts) // LANES) * LANES
     next_hidden = pl.pallas_call(
         functools.partial(expert_kernel, n, readers),
         out_shape=jax.ShapeDtypeStruct((width, seqs), BF16),
         in_specs=vmem(7) + [ANY, ANY],
         out_specs=vmem(1)[0],
         scratch_shapes=[
-            pltpu.VMEM(up_shape, BF16),
+            pltpu.VMEM((1, hidden_units, full_width), BF16),
             pltpu.VMEM(expert_down.shape, BF16),
-            pltpu.VMEM((full_width, seqs), F32),
-            pltpu.VMEM((full_width, seqs), F32),
-            pltpu.VMEM((router_weight.shape[1], full_width), BF16),
-            pltpu.VMEM((router_weight.shape[1], full_width), BF16),
-            pltpu.VMEM((n, kept, LANES), F32),
-            pltpu.VMEM((kept, LANES), F32),
-            piece(n),
+            pltpu.VMEM((n, width, extent), BF16),
+            pltpu.VMEM((n, width, hidden_units), BF16),
             pltpu.VMEM((kept, LANES), BF16),
             piece(n),
-            pltpu.VMEM((seqs, 128), F32),
-            pltpu.VMEM((readers - 1, seqs, 128), F32),
+            pltpu.VMEM((seqs, extent), F32),
+            pltpu.VMEM((last - first, LANES), F32),
+            pltpu.VMEM((kept, LANES), F32),
+            pltpu.VMEM((readers - 1, 8, LANES), F32),
             DMA((2,)),
             DMA((readers - 1,)),
             DMA((readers - 1,)),
@@ -814,13 +793,13 @@
         ]
         + reduce_bufs * 2,
         compiler_params=pltpu.CompilerParams(
-            collective_id=1, has_side_effects=True, vmem_limit_bytes=46 << 20
+            collective_id=1, has_side_effects=True, vmem_limit_bytes=50 << 20
         ),
         name="mix_and_serve",
     )(
-        gated,
-        gated_gain,
-        proj_out,
+        weighted,
+        sums,
+        proj_turned,
         tokens.T,
         moe_gain,
         router_weight.T,

time: 72.6 us -> 63.9 us (0.88)
  Pallas kernels: 68.6 us -> 62.4 us
  local copies, waits for them, and re-layouts: 3.07 us -> 0.65 us
    pallas_call x1, Pallas kernels: 40.6 us -> 34.3 us  [local(): pl.pallas_call(functools.partial(expert_kernel, n, readers), out_shape=ja...]
    unnamed x15 -> x9, local copies, waits for them, and re-layouts: 3.07 us -> 0.65 us
where the time goes in v2:
time: 63.9 us; the launch traced here: 63.7 us
  Pallas kernels  62.4 us (98%)
  between operations  0.7 us (1%)
  local copies, waits for them, and re-layouts  0.65 us (1%)
    pallas_call x1, Pallas kernels, local(): pl.pallas_call(functools.partial(expert_kernel, n, readers), out_shape=ja...  34.3 us
    pallas_call x1, Pallas kernels, local(): pl.pallas_call(functools.partial(gather_kernel, n), out_shape=(pltpu.VMEM...  20.1 us
    pallas_call x1, Pallas kernels, local(): pl.pallas_call(functools.partial(state_kernel, rows, seqs), grid=(seqs //...  7.98 us

profile of v2, /device:TPU:0, one launch (start us, length us, event | category | flops | bytes accessed | tf_op | source)
XLA Modules:
  0.0 63.7 jit_solution(17649249444323807779)
XLA Ops:
  0.6 20.1 %gather_tokens.1 = (f32[96,4,64,128]{3,2,1,0:T(8,128)S(1)}, f32[256,128]{1,0:T(8,128)S(1)}, f32[256,128]{1,0:T(8,128)S(1)}, f32[256,128]{1,0:T(8,128)S(1)}, f32[...) custom-call(bf16[168,96]{1,0:T(8,128)(2,1)} %bitcast.8, ...), custom_call_target="tpu_custom_call" | custom-call | tf_op jit(solution)/shard_map/gather_tokens/pallas_call | solution.py:680
  20.7 0.0 copy-start
  20.7 0.0 copy-start.1
  20.7 0.0 copy-start.2
  20.7 0.0 copy-start.3
  20.8 8.0 %update_state.1 = (f32[96,4,64,128]{3,2,1,0:T(8,128)}, bf16[256,128]{1,0:T(8,128)(2,1)S(1)}, f32[8,128]{1,0:T(8,128)S(1)}) custom-call(f32[96,4,64,128]{3,2,1,0:T(8,128)S(1)} %get-tuple-element.14.state, f32[256,128]{1,0:T(8,128)S(1)} %get-tuple-element.15.columns, f32[256,128]{1,0:T(8,128)S(1)} %get-tuple-element.16.decays, ...), custom_call_target="tpu_custom_call" | custom-call | tf_op jit(solution)/shard_map/update_state/pallas_call | solution.py:734
  28.7 0.0 copy-done
  28.7 0.0 copy-done.1
  28.7 0.0 copy-done.2
  28.7 0.0 copy-done.3
  28.8 34.3 %mix_and_serve.1 = bf16[168,96]{1,0:T(8,128)(2,1)S(1)} custom-call(bf16[256,128]{1,0:T(8,128)(2,1)S(1)} %get-tuple-element.22.weighted, f32[8,128]{1,0:T(8,128)S(1)} %get-tuple-element.23.sums, bf16[16,168,256]{2,1,0:T(8,128)(2,1)S(1)} %get-tuple-element.24.proj_turned, bf16[168,96]{1,0:T(8,128)(2,1)S(1)} %bitcast.9, bf16[2688]{0:T(1024)(128)(2,1)S(1)} %copy-done.2, ...), custom_call_target="tpu_custom_call" | custom-call | tf_op jit(solution)/shard_map/mix_and_serve/pallas_call | solution.py:772
  63.1 0.6 copy.23
Async XLA Ops:
  20.7 8.0 %copy-start = (bf16[96,168]{0,1:T(8,128)(2,1)S(1)}, bf16[96,168]{0,1:T(8,128)(2,1)}, u32[]{:S(2)}) copy-start(bf16[96,168]{0,1:T(8,128)(2,1)} %param.20) | copy-start | bytes 96772
  20.7 8.0 %copy-start.1 = (bf16[2688,16]{0,1:T(8,128)(2,1)S(1)}, bf16[2688,16]{0,1:T(8,128)(2,1)}, u32[]{:S(2)}) copy-start(bf16[2688,16]{0,1:T(8,128)(2,1)} %param.36) | copy-start | bytes 258052
  20.7 8.0 %copy-start.2 = (bf16[2688]{0:T(1024)(128)(2,1)S(1)}, bf16[2688]{0:T(1024)(128)(2,1)}, u32[]{:S(2)}) copy-start(bf16[2688]{0:T(1024)(128)(2,1)} %moe_gain.1) | copy-start | bytes 16132
  20.7 8.0 %copy-start.3 = (s32[96,6]{0,1:T(8,128)S(1)}, s32[96,6]{0,1:T(8,128)}, u32[]{:S(2)}) copy-start(s32[96,6]{0,1:T(8,128)} %param.37) | copy-start | bytes 6916

commit v3 on v2

--- a/solution.py
+++ b/solution.py
@@ -17,20 +17,14 @@
 BF16 = jnp.bfloat16
 
 
-def greet_all(n, me):
-    barrier = pltpu.get_barrier_semaphore()
-
-    def greet(k, carry):
-        pl.semaphore_signal(
-            barrier, inc=1, device_id={"wide": lax.rem(me + k, n)}, device_id_type=MESH
-        )
-        return carry
-
-    lax.fori_loop(1, n, greet, 0)
-
-
-def await_all(n):
-    pl.semaphore_wait(pltpu.get_barrier_semaphore(), n - 1)
+def greet(peer):
+    pl.semaphore_signal(
+        pltpu.get_barrier_semaphore(), inc=1, device_id={"wide": peer}, device_id_type=MESH
+    )
+
+
+def await_peers(count):
+    pl.semaphore_wait(pltpu.get_barrier_semaphore(), count)
 
 
 def place_of(n, me):
@@ -40,12 +34,28 @@
 
 def index_of(line, side, core):
     return line * 4 + side * 2 + core
+
+
+def flipped(line, mask, lines):
+    if lines & (lines - 1):
+        return lax.rem(mask - line + lines, lines)
+    moved, bit = 0, 1
+    while bit < lines:
+        own = lax.rem(line // bit, 2)
+        moved = moved + bit * (1 - own if mask & bit else own)
+        bit *= 2
+    return moved
+
+
+def meetings(lines):
+    return [(mask, turn) for mask in range(lines - 1, -1, -1) for turn in (1, 0) if mask or turn]
 
 
 def gather_all(n, me, own, landing, send_sems, recv_sems, consume, meanwhile=None):
     lines, line, side, core = place_of(n, me)
     across = index_of(line, 1 - side, core)
     partner = index_of(line, side, 1 - core)
+    corner = index_of(line, 1 - side, 1 - core)
     sent = []
 
     def send(src, origin, peer):
@@ -70,41 +80,40 @@
             device_id_type=MESH,
         ).wait_recv()
 
-    for k in range(1, lines):
-        send(own, me, index_of(lax.rem(line + k, lines), side, core))
+    def take(mask, to_side, to_core, peers):
+        origin = index_of(flipped(line, mask, lines), to_side, to_core)
+        arrive(origin)
+        for peer in peers:
+            send(landing.at[origin], origin, peer)
+        consume(landing.at[origin], origin)
+
+    for mask in range(lines - 1, 0, -1):
+        send(own, me, index_of(flipped(line, mask, lines), side, core))
     send(own, me, across)
     send(own, me, partner)
     if meanwhile is not None:
         meanwhile()
     consume(own, me)
-    arrive(partner)
-    consume(landing.at[partner], partner)
-    for k in range(1, lines):
-        origin = index_of(lax.rem(line + lines - k, lines), side, core)
-        arrive(origin)
-        send(landing.at[origin], origin, across)
-        send(landing.at[origin], origin, partner)
-        consume(landing.at[origin], origin)
-    for k in range(lines):
-        origin = index_of(lax.rem(line + lines - k, lines), 1 - side, core)
-        arrive(origin)
-        send(landing.at[origin], origin, partner)
-        consume(landing.at[origin], origin)
-    for other in (side, 1 - side):
-        for k in range(lines):
-            if k == 0 and other is side:
-                continue
-            origin = index_of(lax.rem(line + lines - k, lines), other, 1 - core)
-            arrive(origin)
-            consume(landing.at[origin], origin)
+    take(0, side, 1 - core, [])
+    for mask in range(1, lines):
+        take(mask, side, core, [across, corner, partner] if mask > DIRECT else [across, partner])
+        if mask == 1:
+            take(0, 1 - side, core, [partner])
+    take(1, side, 1 - core, [])
+    take(0, 1 - side, 1 - core, [])
+    for mask in range(1, lines):
+        take(mask, 1 - side, core, [] if mask > DIRECT else [partner])
+        if mask > 1:
+            take(mask, side, 1 - core, [])
+    for mask in range(1, lines):
+        take(mask, 1 - side, 1 - core, [])
     for copy in sent:
         copy.wait_send()
 
 
-def reduce_all(n, me, make, enter, bufs, finish, early, late):
-    outgoing, mine, core_in, side_out, side_in, line_out, line_in, sends, core_sem, side_sem, line_sem = bufs
+def reduce_all(n, me, make, enter, bufs, finish, meanwhile):
+    outgoing, mine, core_in, leaving, coming, sends, core_sem, chip_sem = bufs
     lines, line, side, core = place_of(n, me)
-    across = index_of(line, 1 - side, core)
     partner = index_of(line, side, 1 - core)
     sent = []
 
@@ -126,56 +135,51 @@
     def arrive(dst, sem):
         copy_of(dst, dst, sem, partner, 0).wait_recv()
 
-    def ahead(k):
-        return lax.rem(line + k, lines)
-
-    order = [(k, other) for k in range(1, lines + 1) for other in (1 - side, side)]
+    others = meetings(lines)
+    order = others + [(0, 0)]
+
+    def met(mask, turn, which):
+        return index_of(flipped(line, mask, lines), lax.rem(side + turn, 2), which)
+
+    def fill(number):
+        outgoing[number] = make(met(*order[number], 1 - core)).astype(BF16)
+
+    def keep(number):
+        mine[number] = make(met(*order[number], core))
+
+    numbers = range(len(order))
     if enter is not None:
-        for number, (k, other) in enumerate(order):
-            outgoing[number] = make(index_of(ahead(k), other, 1 - core)).astype(BF16)
+        for number in numbers:
+            fill(number)
+        for number in numbers:
+            keep(number)
         enter()
-    for number, (k, other) in enumerate(order):
+    for number in numbers:
         if enter is None:
-            outgoing[number] = make(index_of(ahead(k), other, 1 - core)).astype(BF16)
+            fill(number)
         send(outgoing.at[number], core_in.at[number], core_sem.at[number], partner)
-    for number, (k, other) in enumerate(order):
-        mine[number] = make(index_of(ahead(k), other, core))
 
     def pair_sum(number):
+        if enter is None:
+            keep(number)
         arrive(core_in.at[number], core_sem.at[number])
         return finish(mine[number] + core_in[number].astype(F32))
 
-    for k in range(1, lines + 1):
-        slot = k - 1
-        side_out[slot] = pair_sum(2 * slot).astype(BF16)
-        send(side_out.at[slot], side_in.at[slot], side_sem.at[slot], across)
-    early()
-
-    def third(k):
-        slot = k - 1
-        value = pair_sum(2 * slot + 1)
-        arrive(side_in.at[slot], side_sem.at[slot])
-        return value + side_in[slot].astype(F32)
-
-    for k in range(1, lines):
-        line_out[k - 1] = third(k).astype(BF16)
-        send(
-            line_out.at[k - 1],
-            line_in.at[k - 1],
-            line_sem.at[k - 1],
-            index_of(ahead(k), side, core),
-        )
-    total = third(lines)
-    late()
-    for k in range(1, lines):
-        arrive(line_in.at[k - 1], line_sem.at[k - 1])
-        total = total + line_in[k - 1].astype(F32)
+    for number, (mask, turn) in enumerate(others):
+        leaving[number] = pair_sum(number).astype(BF16)
+        send(leaving.at[number], coming.at[number], chip_sem.at[number], met(mask, turn, core))
+    total = pair_sum(len(others))
+    meanwhile()
+    for number in reversed(range(len(others))):
+        arrive(coming.at[number], chip_sem.at[number])
+        total = total + coming[number].astype(F32)
     for copy in sent:
         copy.wait_send()
     return total
 
 
 LANES = 128
+DIRECT = 1
 
 
 def packed_shape(width, seqs):
@@ -278,6 +282,8 @@
     proj_hbm,
     gated_gain,
     state,
+    faded_out,
+    packed_out,
     columns_out,
     decays_out,
     skips_out,
@@ -294,6 +300,7 @@
     weights,
     total,
     squares,
+    turned,
     mapped,
     arrived,
     load_sems,
@@ -315,7 +322,30 @@
     load_maps.start()
     load_proj.start()
     load_state.start()
-    greet_all(n, me)
+    lines, line, side, core = place_of(n, me)
+    half = n // 2
+    per_group = half // GROUPS
+    readers = HEADS // GROUPS // heads
+    group = me // readers
+    origins = [
+        (slot // per_group) * half + group * per_group + slot % per_group
+        for slot in range(2 * per_group)
+    ]
+    reader = lax.rem(me, half) // per_group * readers
+    for mask in range(1, lines):
+        greet(index_of(flipped(line, mask, lines), side, core))
+    for turn in (0, 1):
+        greet(index_of(line, 1 - side, (1 - core if turn else core)))
+    greet(index_of(line, side, 1 - core))
+    for origin in origins:
+
+        @pl.when(origin != me)
+        def _():
+            greet(origin)
+
+    expected = lines + 2
+    for r in range(readers):
+        expected = expected + jnp.where(reader + r != me, 1, 0)
     values = padded(tokens[...].astype(F32))
     sums = jnp.sum(values * values, axis=0, keepdims=True)
     scaled = values * own_columns(gain, n, me, width)
@@ -354,7 +384,7 @@
             fresh, weights[origin], (((0,), (0,)), ((), ())), preferred_element_type=F32
         )
 
-    await_all(n)
+    await_peers(expected)
     gather_all(n, me, own, landing, send_sems, recv_sems, consume, prepare)
     scale = token_scale(squares, seqs, n * width)
 
@@ -362,15 +392,11 @@
         return (total[:, at : at + count] * scale).astype(BF16).astype(F32)
 
     mapped[...] = convolved(projected(0, cols), window_maps, taps_maps[...].astype(F32)).astype(BF16)
-    half = n // 2
-    per_group = half // GROUPS
-    readers = HEADS // GROUPS // heads
     kind = me // half
-    own_group = lax.rem(me, half) // per_group
     own_slot = kind * per_group + lax.rem(me, per_group)
 
     def send(r):
-        peer = own_group * readers + r
+        peer = reader + r
         return peer, pltpu.make_async_remote_copy(
             src_ref=mapped,
             dst_ref=arrived.at[own_slot],
@@ -399,26 +425,51 @@
             wide = jnp.where(head_ids == h, ref[h], wide)
         return wide
 
+    small_ids = lax.broadcasted_iota(jnp.int32, (1, heads), 1)
+
+    def small(ref):
+        narrow = jnp.zeros((1, heads), F32)
+        for h in range(heads):
+            narrow = jnp.where(small_ids == h, ref[h], narrow)
+        return narrow
+
     gate = projected(2 * LANES, inner)
     inputs = convolved(projected(2 * LANES + inner, inner), window, taps[...].astype(F32))
     raw = projected(cols, heads)
+    raw = jax.nn.softplus(raw + small(step_bias))
+    decays = jnp.exp(-jnp.exp(small(decay_log)) * raw)
     steps = jnp.zeros((seqs, inner), F32)
     for h in range(heads):
+        decays_out[h] = jnp.broadcast_to(decays[:, h : h + 1], (seqs, LANES))
         steps = jnp.where(head_ids == h, raw[:, h : h + 1], steps)
-    steps = jax.nn.softplus(steps + spread(step_bias))
-    decays = jnp.exp(-jnp.exp(spread(decay_log)) * steps)
 
     def turn(target, value):
         target[:, seqs:] = jnp.zeros((inner, LANES - seqs), F32)
         target[:, :seqs] = value.T
 
-    turn(columns_out, steps * inputs)
-    turn(decays_out, decays)
-    turn(skips_out, spread(skip_gain) * inputs)
+    turn(turned, steps * inputs)
+    moved = turned[...]
+    middle = inner // 2
+    rows = seqs // columns_out.shape[0]
+    ahead = lane_ids(middle) < rows
+    for i in range(columns_out.shape[0]):
+        top = moved[:middle]
+        high, low = halves(top)
+        packed_out[i] = jnp.where(ahead, high, pltpu.roll(low, rows, 1)).astype(BF16)
+        columns_out[i] = moved[middle:]
+        moved = pltpu.roll(moved, LANES - rows, 1)
+    skipped = spread(skip_gain) * inputs
     turn(gates_out, gate * jax.nn.sigmoid(gate))
-    group = me // readers
-    for slot in range(2 * per_group):
-        origin = (slot // per_group) * half + group * per_group + slot % per_group
+    load_state.wait()
+
+    def fade(s, carry):
+        for h in range(heads):
+            part = slice(h * HEAD_DIM, (h + 1) * HEAD_DIM)
+            faded_out[s, part] = (decays_out[h, pl.ds(s, 1), :] * state[s, h]).astype(BF16)
+        return carry
+
+    lax.fori_loop(0, seqs, fade, 0, unroll=4)
+    for slot, origin in enumerate(origins):
 
         @pl.when(origin != me)
         def _():
@@ -432,11 +483,15 @@
             ).wait_recv()
 
     out_out[...] = jnp.zeros_like(out_out)
+    met = jnp.zeros((1, seqs), F32)
     for slot in range(per_group):
         part = slice(slot * cols, (slot + 1) * cols)
         in_out[:, part] = arrived[slot].astype(F32)
-        out_out[part, :seqs] = arrived[per_group + slot].astype(F32).T
-    load_state.wait()
+        readers_turned = arrived[per_group + slot].astype(F32).T
+        out_out[part, :seqs] = readers_turned
+        met = met + jnp.sum(arrived[slot].astype(F32).T * readers_turned, axis=0, keepdims=True)
+    skips_out[:, seqs:] = jnp.zeros((inner, LANES - seqs), F32)
+    skips_out[:, :seqs] = skipped.T + turned[:, :seqs] * met
     for r in range(readers):
         peer, copy = send(r)
 
@@ -446,36 +501,48 @@
 
 
 def state_kernel(
-    rows, seqs, state, columns, decays, skips, gates, in_maps, out_maps, gains, new_state, weighted, sums, total
+    rows, seqs, state, faded, packed, columns, decays, skips, gates, in_maps, out_maps, gains, new_state, weighted, sums, total
 ):
     step = pl.program_id(0)
     heads = state.shape[1]
     first = step * rows
-    back = lax.rem(LANES - first, LANES)
     lane = lax.broadcasted_iota(jnp.int32, (STATE, LANES), 1)
 
     @pl.when(step == 0)
     def _():
         total[...] = jnp.zeros_like(total)
 
-    drive = pltpu.roll(columns[...], back, 1)
-    fade = [pltpu.roll(decays[h * HEAD_DIM : h * HEAD_DIM + 8, :], back, 1) for h in range(heads)]
-    batch = 4
+    drive = packed[step][:, : 2 * rows]
+    middle = drive.shape[0]
+    maps = in_maps[pl.ds(first, rows), :]
+    own = lax.broadcasted_iota(jnp.int32, (rows, STATE), 0)
+    batch = 2
     found = total[...]
     for start in range(0, rows, batch):
-        left, right = [], []
+        picked = []
         for j in range(start, start + batch):
-            maps = in_maps[pl.ds(first + j, 1), :]
-            parts = []
+            one = jnp.where(own == j, maps, 0.0)
+            picked.append(jnp.concatenate([one, one], axis=0))
+        driven = jnp.dot(
+            drive, jnp.concatenate(picked, axis=1).astype(BF16), preferred_element_type=F32
+        )
+        for j in range(start, start + batch):
+            lanes = slice((j - start) * STATE, (j - start + 1) * STATE)
+            row = in_maps[pl.ds(first + j, 1), :]
             for h in range(heads):
-                slow = jnp.broadcast_to(fade[h][:, j : j + 1], (8, LANES))
+                slow = decays[h, pl.ds(first + j, 1), :]
                 for p in range(0, HEAD_DIM, 8):
                     at = h * HEAD_DIM + p
-                    fresh = slow * state[first + j, h, p : p + 8] + drive[at : at + 8, j : j + 1] * maps
-                    new_state[j, h, p : p + 8] = fresh
-                    parts.append(fresh)
-            left.append(jnp.concatenate(parts, axis=0).astype(BF16))
-            right.append(jnp.where(lane == first + j, out_maps[...], 0.0).astype(BF16))
+                    if at < middle:
+                        fresh = driven[at : at + 8, lanes]
+                    else:
+                        fresh = columns[step, at - middle : at - middle + 8, j : j + 1] * row
+                    new_state[j, h, p : p + 8] = slow * state[first + j, h, p : p + 8] + fresh
+        left = [faded[first + j] for j in range(start, start + batch)]
+        right = [
+            jnp.where(lane == first + j, out_maps[...], 0.0).astype(BF16)
+            for j in range(start, start + batch)
+        ]
         found = found + jnp.dot(
             jnp.concatenate(left, axis=1),
             jnp.concatenate(right, axis=0),
@@ -531,9 +598,16 @@
     load_down = pltpu.make_async_copy(down_hbm, down, load_sems.at[1])
     load_up.start()
     load_down.start()
-    greet_all(n, me)
+    lines, line, side, core = place_of(n, me)
     first = (me // partners) * partners
     place = lax.rem(me, partners)
+    others = meetings(lines)
+    for mask, turn in others:
+        greet(index_of(flipped(line, mask, lines), lax.rem(side + turn, 2), core))
+    greet(index_of(line, 1 - side, 1 - core))
+    greet(index_of(line, side, 1 - core))
+    for k in range(1, partners):
+        greet(first + lax.rem(place + k, partners))
 
     def partner_copy(k):
         other = lax.rem(place + k, partners)
@@ -550,7 +624,7 @@
         return pack(jnp.dot(proj_turned[i], weighted[...], preferred_element_type=F32), seqs)
 
     def enter():
-        await_all(n)
+        await_peers(len(others) + 1 + partners)
         for k in range(1, partners):
             partner_copy(k).start()
 
@@ -584,7 +658,7 @@
         pass
 
     half = len(bufs) // 2
-    reduced = reduce_all(n, me, mixed, enter, bufs[:half], scaled, turn_up, nothing)
+    reduced = reduce_all(n, me, mixed, enter, bufs[:half], scaled, turn_up)
     held = pack(padded(tokens[...].astype(F32)), seqs)
     held = (held + reduced).astype(BF16).astype(F32)
     power = held * held
@@ -631,7 +705,7 @@
     def served(i):
         return pack(jnp.dot(down_turned[i], active, preferred_element_type=F32), seqs)
 
-    reduced = reduce_all(n, me, served, None, bufs[half:], lambda value: value, nothing, nothing)
+    reduced = reduce_all(n, me, served, None, bufs[half:], lambda value: value, nothing)
     result[...] = unpack(held + reduced, width, seqs)[:, :seqs].astype(BF16)
 
 
@@ -677,12 +751,15 @@
     first, last = extra_rows(width, seqs)
     across = 2 * LANES + 2 * inner
     scalars = pl.BlockSpec(memory_space=pltpu.SMEM)
-    state, columns, decays, skips, gates, in_maps, out_maps, gains, proj_turned = pl.pallas_call(
+    rows = 16
+    state, faded, packed, columns, decays, skips, gates, in_maps, out_maps, gains, proj_turned = pl.pallas_call(
         functools.partial(gather_kernel, n),
         out_shape=(
             pltpu.VMEM(ssm_state.shape, F32),
-            pltpu.VMEM((inner, LANES), F32),
-            pltpu.VMEM((inner, LANES), F32),
+            pltpu.VMEM((seqs, inner, STATE), BF16),
+            pltpu.VMEM((seqs // rows, inner // 2, LANES), BF16),
+            pltpu.VMEM((seqs // rows, inner // 2, LANES), F32),
+            pltpu.VMEM((heads, seqs, LANES), F32),
             pltpu.VMEM((inner, LANES), F32),
             pltpu.VMEM((inner, LANES), F32),
             pltpu.VMEM((seqs, STATE), F32),
@@ -691,7 +768,7 @@
             pltpu.VMEM((n, width, inner), BF16),
         ),
         in_specs=vmem(2) + [ANY] * 2 + vmem(5) + [scalars] * 3 + [ANY] * 2 + vmem(1),
-        out_specs=tuple(vmem(9)),
+        out_specs=tuple(vmem(11)),
         scratch_shapes=[
             pltpu.VMEM((n, kept, LANES), BF16),
             pltpu.VMEM((kept, LANES), BF16),
@@ -701,6 +778,7 @@
             pltpu.VMEM((n, width, across), BF16),
             pltpu.VMEM((seqs, across), F32),
             pltpu.VMEM((last - first, LANES), F32),
+            pltpu.VMEM((inner, LANES), F32),
             pltpu.VMEM((seqs, cols), BF16),
             pltpu.VMEM((slots, seqs, cols), BF16),
             DMA((4,)),
@@ -710,7 +788,7 @@
             DMA((slots,)),
         ],
         compiler_params=pltpu.CompilerParams(
-            collective_id=0, has_side_effects=True, vmem_limit_bytes=49 << 20
+            collective_id=0, has_side_effects=True, vmem_limit_bytes=42 << 20
         ),
         name="gather_tokens",
     )(
@@ -730,7 +808,6 @@
         proj_out,
         gated_gain,
     )
-    rows = 16
     new_state, weighted, sums = pl.pallas_call(
         functools.partial(state_kernel, rows, seqs),
         grid=(seqs // rows,),
@@ -739,7 +816,7 @@
             pltpu.VMEM((inner, LANES), BF16),
             pltpu.VMEM((8, LANES), F32),
         ),
-        in_specs=vmem(8),
+        in_specs=vmem(10),
         out_specs=(
             pl.BlockSpec((rows, heads, HEAD_DIM, STATE), lambda i: (i, 0, 0, 0)),
             *vmem(2),
@@ -747,24 +824,21 @@
         scratch_shapes=[pltpu.VMEM((inner, LANES), F32)],
         compiler_params=pltpu.CompilerParams(vmem_limit_bytes=16 << 20),
         name="update_state",
-    )(state, columns, decays, skips, gates, in_maps, out_maps, gains)
-    lines = n // 4
+    )(state, faded, packed, columns, decays, skips, gates, in_maps, out_maps, gains)
+    chips = n // 2
 
     def piece(count, kind=BF16):
         return pltpu.VMEM((count, kept, LANES), kind)
 
     reduce_bufs = [
-        piece(2 * lines),
-        piece(2 * lines, F32),
-        piece(2 * lines),
-        piece(lines),
-        piece(lines),
-        piece(lines),
-        piece(lines),
-        DMA((4 * lines - 1,)),
-        DMA((2 * lines,)),
-        DMA((lines,)),
-        DMA((lines,)),
+        piece(chips),
+        piece(chips, F32),
+        piece(chips),
+        piece(chips - 1),
+        piece(chips - 1),
+        DMA((2 * chips - 1,)),
+        DMA((chips,)),
+        DMA((chips - 1,)),
     ]
     hidden_units = expert_up.shape[2]
     experts = router_weight.shape[1]

time: 63.9 us -> 60.5 us (0.947)
  Pallas kernels: 62.4 us -> 59 us
    pallas_call x1, Pallas kernels: 7.98 us -> 6.41 us  [local(): pl.pallas_call(functools.partial(state_kernel, rows, seqs), grid=(seqs //...]
    pallas_call x1, Pallas kernels: 34.3 us -> 33.2 us  [local(): pl.pallas_call(functools.partial(expert_kernel, n, readers), out_shape=ja...]
    pallas_call x1, Pallas kernels: 20.1 us -> 19.3 us  [local(): pl.pallas_call(functools.partial(gather_kernel, n), out_shape=(pltpu.VMEM...]
where the time goes in v3:
time: 60.5 us; the launch traced here: 60.3 us
  Pallas kernels  59 us (98%)
  between operations  0.7 us (1%)
  local copies, waits for them, and re-layouts  0.65 us (1%)
    pallas_call x1, Pallas kernels, local(): pl.pallas_call(functools.partial(expert_kernel, n, readers), out_shape=ja...  33.2 us
    pallas_call x1, Pallas kernels, local(): pl.pallas_call(functools.partial(gather_kernel, n), out_shape=(pltpu.VMEM...  19.3 us
    pallas_call x1, Pallas kernels, local(): pl.pallas_call(functools.partial(state_kernel, rows, seqs), grid=(seqs //...  6.41 us

profile of v3, /device:TPU:0, one launch (start us, length us, event | category | flops | bytes accessed | tf_op | source)
XLA Modules:
  0.0 60.3 jit_solution(9236486337080809007)
XLA Ops:
  0.6 19.3 %gather_tokens.1 = (f32[96,4,64,128]{3,2,1,0:T(8,128)S(1)}, bf16[96,256,128]{2,1,0:T(8,128)(2,1)S(1)}, bf16[6,128,128]{2,1,0:T(8,128)(2,1)S(1)}, f32[6,128,128]{...) custom-call(bf16[168,96]{1,0:T(8,128)(2,1)} %bitcast.8, ...), custom_call_target="tpu_custom_call" | custom-call | tf_op jit(solution)/shard_map/gather_tokens/pallas_call | solution.py:755
  20.0 0.0 copy-start
  20.0 0.0 copy-start.1
  20.0 0.0 copy-start.2
  20.0 0.0 copy-start.3
  20.0 6.4 %update_state.1 = (f32[96,4,64,128]{3,2,1,0:T(8,128)}, bf16[256,128]{1,0:T(8,128)(2,1)S(1)}, f32[8,128]{1,0:T(8,128)S(1)}) custom-call(f32[96,4,64,128]{3,2,1,0:T(8,128)S(1)} %get-tuple-element.16.state, bf16[96,256,128]{2,1,0:T(8,128)(2,1)S(1)} %get-tuple-element.17.faded, bf16[6,128,128]{2,1,0:T(8,128)(2,1)S(1)} %get-tuple-element.18.packed, ...), custom_call_target="tpu_custom_call" | custom-call | tf_op jit(solution)/shard_map/update_state/pallas_call | solution.py:811
  26.4 0.0 copy-done
  26.4 0.0 copy-done.1
  26.5 0.0 copy-done.2
  26.5 0.0 copy-done.3
  26.5 33.2 %mix_and_serve.1 = bf16[168,96]{1,0:T(8,128)(2,1)S(1)} custom-call(bf16[256,128]{1,0:T(8,128)(2,1)S(1)} %get-tuple-element.26.weighted, f32[8,128]{1,0:T(8,128)S(1)} %get-tuple-element.27.sums, bf16[16,168,256]{2,1,0:T(8,128)(2,1)S(1)} %get-tuple-element.28.proj_turned, bf16[168,96]{1,0:T(8,128)(2,1)S(1)} %bitcast.9, bf16[2688]{0:T(1024)(128)(2,1)S(1)} %copy-done.2, ...), custom_call_target="tpu_custom_call" | custom-call | tf_op jit(solution)/shard_map/mix_and_serve/pallas_call | solution.py:846
  59.7 0.6 %copy.23 = bf16[96,168]{0,1:T(8,128)(2,1)} copy(bf16[96,168]{0,1:T(8,128)(2,1)S(1)} %bitcast.10) | data formatting | bytes 64512
Async XLA Ops:
  20.0 6.5 %copy-start = (bf16[96,168]{0,1:T(8,128)(2,1)S(1)}, bf16[96,168]{0,1:T(8,128)(2,1)}, u32[]{:S(2)}) copy-start(bf16[96,168]{0,1:T(8,128)(2,1)} %param.20) | copy-start | bytes 96772
  20.0 6.5 %copy-start.1 = (bf16[2688,16]{0,1:T(8,128)(2,1)S(1)}, bf16[2688,16]{0,1:T(8,128)(2,1)}, u32[]{:S(2)}) copy-start(bf16[2688,16]{0,1:T(8,128)(2,1)} %param.36) | copy-start | bytes 258052
  20.0 6.4 %copy-start.2 = (bf16[2688]{0:T(1024)(128)(2,1)S(1)}, bf16[2688]{0:T(1024)(128)(2,1)}, u32[]{:S(2)}) copy-start(bf16[2688]{0:T(1024)(128)(2,1)} %moe_gain.1) | copy-start | bytes 16132
  20.0 6.4 %copy-start.3 = (s32[96,6]{0,1:T(8,128)S(1)}, s32[96,6]{0,1:T(8,128)}, u32[]{:S(2)}) copy-start(s32[96,6]{0,1:T(8,128)} %param.37) | copy-start | bytes 6916

commit v4 on v3

--- a/solution.py
+++ b/solution.py
@@ -179,7 +179,7 @@
 
 
 LANES = 128
-DIRECT = 1
+DIRECT = 2
 
 
 def packed_shape(width, seqs):
@@ -266,21 +266,21 @@
 
 def gather_kernel(
     n,
-    tokens,
-    gain,
     inner_hbm,
     maps_hbm,
-    step_weights,
-    window,
-    window_maps,
-    taps,
-    taps_maps,
-    step_bias,
-    decay_log,
-    skip_gain,
     state_hbm,
     proj_hbm,
-    gated_gain,
+    tokens_hbm,
+    gain_hbm,
+    step_weights_hbm,
+    window_hbm,
+    window_maps_hbm,
+    taps_hbm,
+    taps_maps_hbm,
+    step_bias_hbm,
+    decay_log_hbm,
+    skip_gain_hbm,
+    gated_gain_hbm,
     state,
     faded_out,
     packed_out,
@@ -294,6 +294,17 @@
     proj_turned,
     landing,
     own,
+    tokens,
+    gain,
+    step_weights,
+    window,
+    window_maps,
+    taps,
+    taps_maps,
+    step_bias,
+    decay_log,
+    skip_gain,
+    gated_gain,
     raw_inner,
     raw_maps,
     raw_proj,
@@ -314,14 +325,6 @@
     inner = window.shape[2]
     cols = window_maps.shape[2]
     heads = step_weights.shape[0]
-    load_inner = pltpu.make_async_copy(inner_hbm, raw_inner, load_sems.at[0])
-    load_maps = pltpu.make_async_copy(maps_hbm, raw_maps, load_sems.at[1])
-    load_state = pltpu.make_async_copy(state_hbm, state, load_sems.at[2])
-    load_proj = pltpu.make_async_copy(proj_hbm, raw_proj, load_sems.at[3])
-    load_inner.start()
-    load_maps.start()
-    load_proj.start()
-    load_state.start()
     lines, line, side, core = place_of(n, me)
     half = n // 2
     per_group = half // GROUPS
@@ -343,9 +346,38 @@
         def _():
             greet(origin)
 
+    small = [
+        (tokens_hbm, tokens),
+        (gain_hbm, gain),
+        (step_weights_hbm, step_weights),
+        (window_hbm, window),
+        (window_maps_hbm, window_maps),
+        (taps_hbm, taps),
+        (taps_maps_hbm, taps_maps),
+        (step_bias_hbm, step_bias),
+        (decay_log_hbm, decay_log),
+        (skip_gain_hbm, skip_gain),
+        (gated_gain_hbm, gated_gain),
+    ]
+    loads = [
+        pltpu.make_async_copy(source, target, load_sems.at[4 + i])
+        for i, (source, target) in enumerate(small)
+    ]
+    for load in loads:
+        load.start()
+    load_inner = pltpu.make_async_copy(inner_hbm, raw_inner, load_sems.at[0])
+    load_maps = pltpu.make_async_copy(maps_hbm, raw_maps, load_sems.at[1])
+    load_state = pltpu.make_async_copy(state_hbm, state, load_sems.at[2])
+    load_proj = pltpu.make_async_copy(proj_hbm, raw_proj, load_sems.at[3])
+    load_inner.start()
+    load_maps.start()
+    load_proj.start()
+    load_state.start()
     expected = lines + 2
     for r in range(readers):
         expected = expected + jnp.where(reader + r != me, 1, 0)
+    loads[0].wait()
+    loads[1].wait()
     values = padded(tokens[...].astype(F32))
     sums = jnp.sum(values * values, axis=0, keepdims=True)
     scaled = values * own_columns(gain, n, me, width)
@@ -355,6 +387,8 @@
     first, last = extra_rows(width, seqs)
 
     def prepare():
+        for load in loads[2:]:
+            load.wait()
         load_inner.wait()
         load_maps.wait()
         steps = step_weights[...].astype(F32).T.astype(BF16)
@@ -422,22 +456,14 @@
     def spread(ref):
         wide = jnp.zeros((1, inner), F32)
         for h in range(heads):
-            wide = jnp.where(head_ids == h, ref[h], wide)
+            wide = jnp.where(head_ids == h, ref[...][None][:, h : h + 1], wide)
         return wide
-
-    small_ids = lax.broadcasted_iota(jnp.int32, (1, heads), 1)
-
-    def small(ref):
-        narrow = jnp.zeros((1, heads), F32)
-        for h in range(heads):
-            narrow = jnp.where(small_ids == h, ref[h], narrow)
-        return narrow
 
     gate = projected(2 * LANES, inner)
     inputs = convolved(projected(2 * LANES + inner, inner), window, taps[...].astype(F32))
     raw = projected(cols, heads)
-    raw = jax.nn.softplus(raw + small(step_bias))
-    decays = jnp.exp(-jnp.exp(small(decay_log)) * raw)
+    raw = jax.nn.softplus(raw + step_bias[...][None])
+    decays = jnp.exp(-jnp.exp(decay_log[...][None]) * raw)
     steps = jnp.zeros((seqs, inner), F32)
     for h in range(heads):
         decays_out[h] = jnp.broadcast_to(decays[:, h : h + 1], (seqs, LANES))
@@ -501,60 +527,85 @@
 
 
 def state_kernel(
-    rows, seqs, state, faded, packed, columns, decays, skips, gates, in_maps, out_maps, gains, new_state, weighted, sums, total
+    rows,
+    seqs,
+    state,
+    faded,
+    packed,
+    columns,
+    decays,
+    skips,
+    gates,
+    in_maps,
+    out_maps,
+    gains,
+    new_state,
+    weighted,
+    sums,
+    fresh,
+    total,
+    store_sems,
 ):
-    step = pl.program_id(0)
     heads = state.shape[1]
-    first = step * rows
     lane = lax.broadcasted_iota(jnp.int32, (STATE, LANES), 1)
-
-    @pl.when(step == 0)
-    def _():
-        total[...] = jnp.zeros_like(total)
-
-    drive = packed[step][:, : 2 * rows]
-    middle = drive.shape[0]
-    maps = in_maps[pl.ds(first, rows), :]
     own = lax.broadcasted_iota(jnp.int32, (rows, STATE), 0)
+    slots, part = fresh.shape[:2]
+    middle = packed.shape[1]
     batch = 2
-    found = total[...]
-    for start in range(0, rows, batch):
+    copies = []
+    for start in range(0, seqs, batch):
+        step, first = divmod(start, rows)
+        chunk, place = divmod(start, part)
+        slot = chunk % slots
+        if place == 0 and chunk >= slots:
+            copies[chunk - slots].wait()
         picked = []
-        for j in range(start, start + batch):
+        maps = in_maps[step * rows : (step + 1) * rows, :]
+        for j in range(first, first + batch):
             one = jnp.where(own == j, maps, 0.0)
             picked.append(jnp.concatenate([one, one], axis=0))
         driven = jnp.dot(
-            drive, jnp.concatenate(picked, axis=1).astype(BF16), preferred_element_type=F32
+            packed[step][:, : 2 * rows],
+            jnp.concatenate(picked, axis=1).astype(BF16),
+            preferred_element_type=F32,
         )
-        for j in range(start, start + batch):
-            lanes = slice((j - start) * STATE, (j - start + 1) * STATE)
-            row = in_maps[pl.ds(first + j, 1), :]
+        for i in range(batch):
+            lanes = slice(i * STATE, (i + 1) * STATE)
+            row = in_maps[start + i : start + i + 1, :]
             for h in range(heads):
-                slow = decays[h, pl.ds(first + j, 1), :]
+                slow = decays[h, start + i : start + i + 1, :]
                 for p in range(0, HEAD_DIM, 8):
                     at = h * HEAD_DIM + p
                     if at < middle:
-                        fresh = driven[at : at + 8, lanes]
+                        drive = driven[at : at + 8, lanes]
                     else:
-                        fresh = columns[step, at - middle : at - middle + 8, j : j + 1] * row
-                    new_state[j, h, p : p + 8] = slow * state[first + j, h, p : p + 8] + fresh
-        left = [faded[first + j] for j in range(start, start + batch)]
+                        to = at - middle
+                        drive = columns[step, to : to + 8, first + i : first + i + 1] * row
+                    value = slow * state[start + i, h, p : p + 8] + drive
+                    fresh[slot, place + i, h, p : p + 8] = value
+        left = [faded[start + i] for i in range(batch)]
         right = [
-            jnp.where(lane == first + j, out_maps[...], 0.0).astype(BF16)
-            for j in range(start, start + batch)
+            jnp.where(lane == start + i, out_maps[...], 0.0).astype(BF16) for i in range(batch)
         ]
-        found = found + jnp.dot(
+        found = jnp.dot(
             jnp.concatenate(left, axis=1),
             jnp.concatenate(right, axis=0),
             preferred_element_type=F32,
         )
-    total[...] = found
-
-    @pl.when(step == pl.num_programs(0) - 1)
-    def _():
-        gated = (total[...] + skips[...]) * gates[...]
-        sums[...] = jnp.broadcast_to(jnp.sum(gated * gated, axis=0, keepdims=True), sums.shape)
-        weighted[...] = (gated * gains[...]).astype(BF16)
+        if start:
+            found = found + total[...]
+        total[...] = found
+        if place + batch == part:
+            copy = pltpu.make_async_copy(
+                fresh.at[slot], new_state.at[pl.ds(chunk * part, part)], store_sems.at[slot]
+            )
+            copy.start()
+            copies.append(copy)
+    gated = (total[...] + skips[...]) * gates[...]
+    sums[...] = jnp.broadcast_to(jnp.sum(gated * gated, axis=0, keepdims=True), sums.shape)
+    weighted[...] = (gated * gains[...]).astype(BF16)
+    for copy in copies[-slots:]:
+        copy.wait()
 
 
 def expert_kernel(
@@ -594,10 +645,6 @@
     extent = up_turned.shape[2]
     kept, rest, gap = packed_shape(width, seqs)
     chunks = seqs // gap
-    load_up = pltpu.make_async_copy(up_hbm, up, load_sems.at[0])
-    load_down = pltpu.make_async_copy(down_hbm, down, load_sems.at[1])
-    load_up.start()
-    load_down.start()
     lines, line, side, core = place_of(n, me)
     first = (me // partners) * partners
     place = lax.rem(me, partners)
@@ -608,6 +655,11 @@
     greet(index_of(line, side, 1 - core))
     for k in range(1, partners):
         greet(first + lax.rem(place + k, partners))
+
+    load_up = pltpu.make_async_copy(up_hbm, up, load_sems.at[0])
+    load_down = pltpu.make_async_copy(down_hbm, down, load_sems.at[1])
+    load_up.start()
+    load_down.start()
 
     def partner_copy(k):
         other = lax.rem(place + k, partners)
@@ -750,7 +802,19 @@
     kept = packed_shape(width, seqs)[0]
     first, last = extra_rows(width, seqs)
     across = 2 * LANES + 2 * inner
-    scalars = pl.BlockSpec(memory_space=pltpu.SMEM)
+    small = (
+        tokens.T,
+        mix_gain,
+        proj_step.T,
+        window_inner.transpose(1, 0, 2),
+        window_maps.transpose(1, 0, 2),
+        kernel_inner,
+        kernel_maps,
+        step_bias,
+        decay_log,
+        skip_gain,
+        gated_gain,
+    )
     rows = 16
     state, faded, packed, columns, decays, skips, gates, in_maps, out_maps, gains, proj_turned = pl.pallas_call(
         functools.partial(gather_kernel, n),
@@ -767,11 +831,12 @@
             pltpu.VMEM((inner, LANES), F32),
             pltpu.VMEM((n, width, inner), BF16),
         ),
-        in_specs=vmem(2) + [ANY] * 2 + vmem(5) + [scalars] * 3 + [ANY] * 2 + vmem(1),
+        in_specs=[ANY] * 15,
         out_specs=tuple(vmem(11)),
         scratch_shapes=[
             pltpu.VMEM((n, kept, LANES), BF16),
             pltpu.VMEM((kept, LANES), BF16),
+            *(pltpu.VMEM(value.shape, value.dtype) for value in small),
             pltpu.VMEM((full_width, 2, inner), BF16),
             pltpu.VMEM((full_width, cols), BF16),
             pltpu.VMEM((inner, full_width), BF16),
@@ -781,7 +846,7 @@
             pltpu.VMEM((inner, LANES), F32),
             pltpu.VMEM((seqs, cols), BF16),
             pltpu.VMEM((slots, seqs, cols), BF16),
-            DMA((4,)),
+            DMA((4 + len(small),)),
             DMA((n,)),
             DMA((n,)),
             DMA((readers,)),
@@ -791,37 +856,21 @@
             collective_id=0, has_side_effects=True, vmem_limit_bytes=42 << 20
         ),
         name="gather_tokens",
-    )(
-        tokens.T,
-        mix_gain,
-        proj_inner,
-        proj_maps,
-        proj_step.T,
-        window_inner.transpose(1, 0, 2),
-        window_maps.transpose(1, 0, 2),
-        kernel_inner,
-        kernel_maps,
-        step_bias,
-        decay_log,
-        skip_gain,
-        ssm_state,
-        proj_out,
-        gated_gain,
-    )
+    )(proj_inner, proj_maps, ssm_state, proj_out, *small)
     new_state, weighted, sums = pl.pallas_call(
         functools.partial(state_kernel, rows, seqs),
-        grid=(seqs // rows,),
         out_shape=(
             jax.ShapeDtypeStruct(ssm_state.shape, F32),
             pltpu.VMEM((inner, LANES), BF16),
             pltpu.VMEM((8, LANES), F32),
         ),
         in_specs=vmem(10),
-        out_specs=(
-            pl.BlockSpec((rows, heads, HEAD_DIM, STATE), lambda i: (i, 0, 0, 0)),
-            *vmem(2),
-        ),
-        scratch_shapes=[pltpu.VMEM((inner, LANES), F32)],
+        out_specs=(ANY, *vmem(2)),
+        scratch_shapes=[
+            pltpu.VMEM((4, 8, heads, HEAD_DIM, STATE), F32),
+            pltpu.VMEM((inner, LANES), F32),
+            DMA((4,)),
+        ],
         compiler_params=pltpu.CompilerParams(vmem_limit_bytes=16 << 20),
         name="update_state",
     )(state, faded, packed, columns, decays, skips, gates, in_maps, out_maps, gains)

time: 60.5 us -> 57.8 us (0.955)
  Pallas kernels: 59 us -> 56.3 us
    pallas_call x1, Pallas kernels: 6.41 us -> 5.13 us  [local(): pl.pallas_call(functools.partial(state_kernel, rows, seqs), out_shape=(ja...]
    pallas_call x1, Pallas kernels: 33.2 us -> 32.3 us  [local(): pl.pallas_call(functools.partial(expert_kernel, n, readers), out_shape=ja...]
where the time goes in v4:
time: 57.8 us; the launch traced here: 57.7 us
  Pallas kernels  56.3 us (97%)
  between operations  0.72 us (1%)
  local copies, waits for them, and re-layouts  0.65 us (1%)
    pallas_call x1, Pallas kernels, local(): pl.pallas_call(functools.partial(expert_kernel, n, readers), out_shape=ja...  32.3 us
    pallas_call x1, Pallas kernels, local(): pl.pallas_call(functools.partial(gather_kernel, n), out_shape=(pltpu.VMEM...  18.8 us
    pallas_call x1, Pallas kernels, local(): pl.pallas_call(functools.partial(state_kernel, rows, seqs), out_shape=(ja...  5.13 us

profile of v4, /device:TPU:0, one launch (start us, length us, event | category | flops | bytes accessed | tf_op | source)
XLA Modules:
  0.0 57.7 jit_solution(9213201624857141813)
XLA Ops:
  0.6 18.8 %gather_tokens.1 = (f32[96,4,64,128]{3,2,1,0:T(8,128)S(1)}, bf16[96,256,128]{2,1,0:T(8,128)(2,1)S(1)}, bf16[6,128,128]{2,1,0:T(8,128)(2,1)S(1)}, f32[6,128,128]{...) custom-call(bf16[2688,2,256]{2,1,0:T(2,128)(2,1)} %inner_hbm.1, ...), custom_call_target="tpu_custom_call" | custom-call | tf_op jit(solution)/shard_map/gather_tokens/pallas_call | solution.py:819
  19.5 0.0 copy-start
  19.5 0.0 copy-start.1
  19.5 0.0 copy-start.2
  19.5 0.0 copy-start.3
  19.5 5.1 %update_state.1 = (f32[96,4,64,128]{3,2,1,0:T(8,128)}, bf16[256,128]{1,0:T(8,128)(2,1)S(1)}, f32[8,128]{1,0:T(8,128)S(1)}) custom-call(f32[96,4,64,128]{3,2,1,0:T(8,128)S(1)} %get-tuple-element.16.state, bf16[96,256,128]{2,1,0:T(8,128)(2,1)S(1)} %get-tuple-element.17.faded, bf16[6,128,128]{2,1,0:T(8,128)(2,1)S(1)} %get-tuple-element.18.packed, ...), custom_call_target="tpu_custom_call" | custom-call | tf_op jit(solution)/shard_map/update_state/pallas_call | solution.py:860
  24.7 0.0 copy-done
  24.7 0.0 copy-done.1
  24.7 0.0 copy-done.2
  24.7 0.0 copy-done.3
  24.7 32.3 %mix_and_serve.1 = bf16[168,96]{1,0:T(8,128)(2,1)S(1)} custom-call(bf16[256,128]{1,0:T(8,128)(2,1)S(1)} %get-tuple-element.26.weighted, f32[8,128]{1,0:T(8,128)S(1)} %get-tuple-element.27.sums, bf16[16,168,256]{2,1,0:T(8,128)(2,1)S(1)} %get-tuple-element.28.proj_turned, bf16[168,96]{1,0:T(8,128)(2,1)S(1)} %bitcast.9, bf16[2688]{0:T(1024)(128)(2,1)S(1)} %copy-done.2, ...), custom_call_target="tpu_custom_call" | custom-call | tf_op jit(solution)/shard_map/mix_and_serve/pallas_call | solution.py:895
  57.1 0.6 %copy.23 = bf16[96,168]{0,1:T(8,128)(2,1)} copy(bf16[96,168]{0,1:T(8,128)(2,1)S(1)} %bitcast.10) | data formatting | bytes 64512
Async XLA Ops:
  19.5 5.2 %copy-start = (bf16[96,168]{0,1:T(8,128)(2,1)S(1)}, bf16[96,168]{0,1:T(8,128)(2,1)}, u32[]{:S(2)}) copy-start(bf16[96,168]{0,1:T(8,128)(2,1)} %param.20) | copy-start | bytes 96772
  19.5 5.2 %copy-start.1 = (bf16[2688,16]{0,1:T(8,128)(2,1)S(1)}, bf16[2688,16]{0,1:T(8,128)(2,1)}, u32[]{:S(2)}) copy-start(bf16[2688,16]{0,1:T(8,128)(2,1)} %param.36) | copy-start | bytes 258052
  19.5 5.2 %copy-start.2 = (bf16[2688]{0:T(1024)(128)(2,1)S(1)}, bf16[2688]{0:T(1024)(128)(2,1)}, u32[]{:S(2)}) copy-start(bf16[2688]{0:T(1024)(128)(2,1)} %moe_gain.1) | copy-start | bytes 16132
  19.5 5.2 %copy-start.3 = (s32[96,6]{0,1:T(8,128)S(1)}, s32[96,6]{0,1:T(8,128)}, u32[]{:S(2)}) copy-start(s32[96,6]{0,1:T(8,128)} %param.37) | copy-start | bytes 6916

commit v5 on v4

--- a/solution.py
+++ b/solution.py
@@ -111,7 +111,7 @@
         copy.wait_send()
 
 
-def reduce_all(n, me, make, enter, bufs, finish, meanwhile):
+def reduce_all(n, me, make, enter, bufs, finish, meanwhile, together=2):
     outgoing, mine, core_in, leaving, coming, sends, core_sem, chip_sem = bufs
     lines, line, side, core = place_of(n, me)
     partner = index_of(line, side, 1 - core)
@@ -141,26 +141,37 @@
     def met(mask, turn, which):
         return index_of(flipped(line, mask, lines), lax.rem(side + turn, 2), which)
 
+    def group(number):
+        return range(number, min(number + together, len(order)))
+
     def fill(number):
-        outgoing[number] = make(met(*order[number], 1 - core)).astype(BF16)
+        blocks = make([met(*order[each], 1 - core) for each in group(number)])
+        for each, block in zip(group(number), blocks):
+            outgoing[each] = block.astype(BF16)
 
     def keep(number):
-        mine[number] = make(met(*order[number], core))
+        blocks = make([met(*order[each], core) for each in group(number)])
+        for each, block in zip(group(number), blocks):
+            mine[each] = block
 
     numbers = range(len(order))
     if enter is not None:
-        for number in numbers:
+        for number in numbers[::together]:
             fill(number)
-        for number in numbers:
+        for number in numbers[::together]:
             keep(number)
         enter()
-    for number in numbers:
-        if enter is None:
+    def give(number):
+        if enter is None and number % together == 0:
             fill(number)
         send(outgoing.at[number], core_in.at[number], core_sem.at[number], partner)
 
+    ahead = len(order) if enter is not None else min(AHEAD, len(order))
+    for number in range(ahead):
+        give(number)
+
     def pair_sum(number):
-        if enter is None:
+        if enter is None and number % together == 0:
             keep(number)
         arrive(core_in.at[number], core_sem.at[number])
         return finish(mine[number] + core_in[number].astype(F32))
@@ -168,6 +179,9 @@
     for number, (mask, turn) in enumerate(others):
         leaving[number] = pair_sum(number).astype(BF16)
         send(leaving.at[number], coming.at[number], chip_sem.at[number], met(mask, turn, core))
+        if (number + 1) % together == 0:
+            for later in group(number + 1 - together + ahead):
+                give(later)
     total = pair_sum(len(others))
     meanwhile()
     for number in reversed(range(len(others))):
@@ -180,6 +194,7 @@
 
 LANES = 128
 DIRECT = 2
+AHEAD = 4
 
 
 def packed_shape(width, seqs):
@@ -672,8 +687,13 @@
             device_id_type=MESH,
         )
 
-    def mixed(i):
-        return pack(jnp.dot(proj_turned[i], weighted[...], preferred_element_type=F32), seqs)
+    def products(turned, blocks, right):
+        tall = jnp.concatenate([turned[i] for i in blocks], axis=0)
+        found = jnp.dot(tall, right, preferred_element_type=F32)
+        return [pack(found[k * width : (k + 1) * width], seqs) for k in range(len(blocks))]
+
+    def mixed(blocks):
+        return products(proj_turned, blocks, weighted[...])
 
     def enter():
         await_peers(len(others) + 1 + partners)
@@ -754,8 +774,8 @@
     active = jnp.concatenate([active, jnp.zeros((LANES - seqs, hidden_units), F32)], axis=0)
     active = active.astype(BF16).T
 
-    def served(i):
-        return pack(jnp.dot(down_turned[i], active, preferred_element_type=F32), seqs)
+    def served(blocks):
+        return products(down_turned, blocks, active)
 
     reduced = reduce_all(n, me, served, None, bufs[half:], lambda value: value, nothing)
     result[...] = unpack(held + reduced, width, seqs)[:, :seqs].astype(BF16)

time: 57.8 us -> 56.7 us (0.981)
  Pallas kernels: 56.3 us -> 55.2 us
    pallas_call x1, Pallas kernels: 32.3 us -> 31.2 us  [local(): pl.pallas_call(functools.partial(expert_kernel, n, readers), out_shape=ja...]
where the time goes in v5:
time: 56.7 us; the launch traced here: 56.5 us
  Pallas kernels  55.2 us (97%)
  between operations  0.72 us (1%)
  local copies, waits for them, and re-layouts  0.65 us (1%)
    pallas_call x1, Pallas kernels, local(): pl.pallas_call(functools.partial(expert_kernel, n, readers), out_shape=ja...  31.2 us
    pallas_call x1, Pallas kernels, local(): pl.pallas_call(functools.partial(gather_kernel, n), out_shape=(pltpu.VMEM...  18.8 us
    pallas_call x1, Pallas kernels, local(): pl.pallas_call(functools.partial(state_kernel, rows, seqs), out_shape=(ja...  5.13 us

profile of v5, /device:TPU:0, one launch (start us, length us, event | category | flops | bytes accessed | tf_op | source)
XLA Modules:
  0.0 56.5 jit_solution(178651448658587887)
XLA Ops:
  0.6 18.8 %gather_tokens.1 = (f32[96,4,64,128]{3,2,1,0:T(8,128)S(1)}, bf16[96,256,128]{2,1,0:T(8,128)(2,1)S(1)}, bf16[6,128,128]{2,1,0:T(8,128)(2,1)S(1)}, f32[6,128,128]{...) custom-call(bf16[2688,2,256]{2,1,0:T(2,128)(2,1)} %inner_hbm.1, ...), custom_call_target="tpu_custom_call" | custom-call | tf_op jit(solution)/shard_map/gather_tokens/pallas_call | solution.py:839
  19.5 0.0 copy-start
  19.5 0.0 copy-start.1
  19.5 0.0 copy-start.2
  19.5 0.0 copy-start.3
  19.5 5.1 %update_state.1 = (f32[96,4,64,128]{3,2,1,0:T(8,128)}, bf16[256,128]{1,0:T(8,128)(2,1)S(1)}, f32[8,128]{1,0:T(8,128)S(1)}) custom-call(f32[96,4,64,128]{3,2,1,0:T(8,128)S(1)} %get-tuple-element.16.state, bf16[96,256,128]{2,1,0:T(8,128)(2,1)S(1)} %get-tuple-element.17.faded, bf16[6,128,128]{2,1,0:T(8,128)(2,1)S(1)} %get-tuple-element.18.packed, ...), custom_call_target="tpu_custom_call" | custom-call | tf_op jit(solution)/shard_map/update_state/pallas_call | solution.py:880
  24.7 0.0 copy-done
  24.7 0.0 copy-done.1
  24.7 0.0 copy-done.2
  24.7 0.0 copy-done.3
  24.7 31.2 %mix_and_serve.1 = bf16[168,96]{1,0:T(8,128)(2,1)S(1)} custom-call(bf16[256,128]{1,0:T(8,128)(2,1)S(1)} %get-tuple-element.26.weighted, f32[8,128]{1,0:T(8,128)S(1)} %get-tuple-element.27.sums, bf16[16,168,256]{2,1,0:T(8,128)(2,1)S(1)} %get-tuple-element.28.proj_turned, bf16[168,96]{1,0:T(8,128)(2,1)S(1)} %bitcast.9, bf16[2688]{0:T(1024)(128)(2,1)S(1)} %copy-done.2, ...), custom_call_target="tpu_custom_call" | custom-call | tf_op jit(solution)/shard_map/mix_and_serve/pallas_call | solution.py:915
  55.9 0.6 %copy.23 = bf16[96,168]{0,1:T(8,128)(2,1)} copy(bf16[96,168]{0,1:T(8,128)(2,1)S(1)} %bitcast.10) | data formatting | bytes 64512
Async XLA Ops:
  19.5 5.2 %copy-start = (bf16[96,168]{0,1:T(8,128)(2,1)S(1)}, bf16[96,168]{0,1:T(8,128)(2,1)}, u32[]{:S(2)}) copy-start(bf16[96,168]{0,1:T(8,128)(2,1)} %param.20) | copy-start | bytes 96772
  19.5 5.2 %copy-start.1 = (bf16[2688,16]{0,1:T(8,128)(2,1)S(1)}, bf16[2688,16]{0,1:T(8,128)(2,1)}, u32[]{:S(2)}) copy-start(bf16[2688,16]{0,1:T(8,128)(2,1)} %param.36) | copy-start | bytes 258052
  19.5 5.2 %copy-start.2 = (bf16[2688]{0:T(1024)(128)(2,1)S(1)}, bf16[2688]{0:T(1024)(128)(2,1)}, u32[]{:S(2)}) copy-start(bf16[2688]{0:T(1024)(128)(2,1)} %moe_gain.1) | copy-start | bytes 16132
  19.5 5.2 %copy-start.3 = (s32[96,6]{0,1:T(8,128)S(1)}, s32[96,6]{0,1:T(8,128)}, u32[]{:S(2)}) copy-start(s32[96,6]{0,1:T(8,128)} %param.37) | copy-start | bytes 6916

commit v6 on v5

--- a/solution.py
+++ b/solution.py
@@ -730,7 +730,7 @@
         pass
 
     half = len(bufs) // 2
-    reduced = reduce_all(n, me, mixed, enter, bufs[:half], scaled, turn_up)
+    reduced = reduce_all(n, me, mixed, enter, bufs[:half], scaled, turn_up, 4)
     held = pack(padded(tokens[...].astype(F32)), seqs)
     held = (held + reduced).astype(BF16).astype(F32)
     power = held * held

time: 56.7 us -> 56.7 us (level)
  no operation moved by 1% of the time
where the time goes in v6:
time: 56.7 us; the launch traced here: 56.5 us
  Pallas kernels  55.2 us (97%)
  between operations  0.72 us (1%)
  local copies, waits for them, and re-layouts  0.65 us (1%)
    pallas_call x1, Pallas kernels, local(): pl.pallas_call(functools.partial(expert_kernel, n, readers), out_shape=ja...  31.2 us
    pallas_call x1, Pallas kernels, local(): pl.pallas_call(functools.partial(gather_kernel, n), out_shape=(pltpu.VMEM...  18.8 us
    pallas_call x1, Pallas kernels, local(): pl.pallas_call(functools.partial(state_kernel, rows, seqs), out_shape=(ja...  5.13 us

profile of v6, /device:TPU:0, one launch (start us, length us, event | category | flops | bytes accessed | tf_op | source)
XLA Modules:
  0.0 56.5 jit_solution(8996285645498149654)
XLA Ops:
  0.6 18.8 %gather_tokens.1 = (f32[96,4,64,128]{3,2,1,0:T(8,128)S(1)}, bf16[96,256,128]{2,1,0:T(8,128)(2,1)S(1)}, bf16[6,128,128]{2,1,0:T(8,128)(2,1)S(1)}, f32[6,128,128]{...) custom-call(bf16[2688,2,256]{2,1,0:T(2,128)(2,1)} %inner_hbm.1, ...), custom_call_target="tpu_custom_call" | custom-call | tf_op jit(solution)/shard_map/gather_tokens/pallas_call | solution.py:839
  19.5 0.0 copy-start
  19.5 0.0 copy-start.1
  19.5 0.0 copy-start.2
  19.5 0.0 copy-start.3
  19.5 5.1 %update_state.1 = (f32[96,4,64,128]{3,2,1,0:T(8,128)}, bf16[256,128]{1,0:T(8,128)(2,1)S(1)}, f32[8,128]{1,0:T(8,128)S(1)}) custom-call(f32[96,4,64,128]{3,2,1,0:T(8,128)S(1)} %get-tuple-element.16.state, bf16[96,256,128]{2,1,0:T(8,128)(2,1)S(1)} %get-tuple-element.17.faded, bf16[6,128,128]{2,1,0:T(8,128)(2,1)S(1)} %get-tuple-element.18.packed, ...), custom_call_target="tpu_custom_call" | custom-call | tf_op jit(solution)/shard_map/update_state/pallas_call | solution.py:880
  24.7 0.0 copy-done
  24.7 0.0 copy-done.1
  24.7 0.0 copy-done.2
  24.7 0.0 copy-done.3
  24.7 31.2 %mix_and_serve.1 = bf16[168,96]{1,0:T(8,128)(2,1)S(1)} custom-call(bf16[256,128]{1,0:T(8,128)(2,1)S(1)} %get-tuple-element.26.weighted, f32[8,128]{1,0:T(8,128)S(1)} %get-tuple-element.27.sums, bf16[16,168,256]{2,1,0:T(8,128)(2,1)S(1)} %get-tuple-element.28.proj_turned, bf16[168,96]{1,0:T(8,128)(2,1)S(1)} %bitcast.9, bf16[2688]{0:T(1024)(128)(2,1)S(1)} %copy-done.2, ...), custom_call_target="tpu_custom_call" | custom-call | tf_op jit(solution)/shard_map/mix_and_serve/pallas_call | solution.py:915
  55.9 0.6 %copy.23 = bf16[96,168]{0,1:T(8,128)(2,1)} copy(bf16[96,168]{0,1:T(8,128)(2,1)S(1)} %bitcast.10) | data formatting | bytes 64512
Async XLA Ops:
  19.5 5.2 %copy-start = (bf16[96,168]{0,1:T(8,128)(2,1)S(1)}, bf16[96,168]{0,1:T(8,128)(2,1)}, u32[]{:S(2)}) copy-start(bf16[96,168]{0,1:T(8,128)(2,1)} %param.20) | copy-start | bytes 96772
  19.5 5.2 %copy-start.1 = (bf16[2688,16]{0,1:T(8,128)(2,1)S(1)}, bf16[2688,16]{0,1:T(8,128)(2,1)}, u32[]{:S(2)}) copy-start(bf16[2688,16]{0,1:T(8,128)(2,1)} %param.36) | copy-start | bytes 258052
  19.5 5.2 %copy-start.2 = (bf16[2688]{0:T(1024)(128)(2,1)S(1)}, bf16[2688]{0:T(1024)(128)(2,1)}, u32[]{:S(2)}) copy-start(bf16[2688]{0:T(1024)(128)(2,1)} %moe_gain.1) | copy-start | bytes 16132
  19.5 5.2 %copy-start.3 = (s32[96,6]{0,1:T(8,128)S(1)}, s32[96,6]{0,1:T(8,128)}, u32[]{:S(2)}) copy-start(s32[96,6]{0,1:T(8,128)} %param.37) | copy-start | bytes 6916
